TPU v7x, 32 devices: a whole 2x2x4 slice. The times are simulated.
32 devices in a mesh: band: 2 (over y), tm: 4 (over z), rows: 4 (over x, core).
Axes of the slice: x: 2, y: 2, z: 4, core: 2. Of those that a mesh axis runs over, the one named last changes fastest.
Arguments:
- recording: bfloat16 [4096, 64, 512], P('tm', ('band', 'rows')), parts along dimension 1, may hold values from -3 to 3
- traces: bfloat16 [128, 4096], P('band', 'tm'), parts along dimension 0, as said below
- footprints: float32 [64, 64, 512], P(None, ('band', 'rows')), parts along dimension 1, may hold values from 0 to 1
- correlation: float32 [64, 512], P(('band', 'rows')), parts along dimension 0, may hold values from 0.5 to 1
- support: int32 [128, 4], P('band'), parts along dimension 0, may hold values from 0 to 7, all different within a row
Outputs:
- renewed: float32 [64, 64, 512], P(None, ('band', 'rows')), parts along dimension 1
There are 2 independent parts, one for each index of `band`. A program takes and returns all parts, laid end to end along the dimension named above; each array names one. Nothing has to cross between parts.
Inputs may be any that keep to these rules, and one draw needn't show every extreme that they name: traces are nonzero reals of magnitude at most 32 / sqrt(4096). `support`: each component names 4 different row tiles; every tile is named by some component.
All inputs are finite; a program needn't handle non-finite values.
Results may differ from a plain program's by a relative error of at most 0.0003.
Values sent between devices are 32-bit elements; how exact they have to be, the bound alone decides.
No kernel may reach another device: no remote copies, remote signals or barrier semaphores. Data moves between devices by JAX's collectives and lax.ppermute only.
A program may use at most 64 MiB of HBM per device.

v0:
```python
import jax
import jax.numpy as jnp
from jax import lax
from jax.sharding import PartitionSpec as P

TILE = 4
PASSES = 4


diffusion_rate = 0.24
step_scale = 0.5
epsilon = 1e-06


def extended_2(block, sides, width):
    for axis, dim in sides:
        count = lax.axis_size(axis)
        forward = [(i, i + 1) for i in range(count - 1)]
        backward = [(target, source) for source, target in forward]
        low = lax.ppermute(
            lax.slice_in_dim(block, block.shape[dim] - width, None, axis=dim), axis, forward
        )
        high = lax.ppermute(lax.slice_in_dim(block, 0, width, axis=dim), axis, backward)
        block = jnp.concatenate([low, block, high], axis=dim)
    return block


def relax_once(center, above, below, weight):
    side_pad = jnp.pad(center, ((0, 0), (0, 0), (1, 1)))
    beside_all = above + below + side_pad[:, :, 2:] + side_pad[:, :, :-2]
    return center + diffusion_rate * weight * (beside_all - 4.0 * center)


def spread(field, correlation):
    stacked = jnp.concatenate([field, correlation[None]], axis=0)
    extended = extended_2(stacked, (("rows", 1),), PASSES)
    current = extended[:-1]
    weights = extended[-1]
    row_total = weights.shape[0]
    for pass_index in range(PASSES):
        weight = weights[pass_index + 1 : row_total - pass_index - 1]
        current = relax_once(current[:, 1:-1], current[:, :-2], current[:, 2:], weight[None])
    return current


def descend(owned, all_flat, gram_matrix, projected, diagonal, owned_mask):
    gradient = (
        jnp.dot(
            gram_matrix,
            all_flat,
            precision=lax.Precision.HIGHEST,
            preferred_element_type=jnp.float32,
        )
        - projected
    )
    updated = owned.reshape(gradient.shape) - step_scale * gradient / (diagonal[:, None] + epsilon)
    return jnp.maximum(updated, 0.0).reshape(owned.shape) * owned_mask[:, :, None]


def per_device(recording, traces, footprints, correlation, support):
    frame_count, row_count, col_count = recording.shape
    components = traces.shape[0]
    flattened = recording.reshape(frame_count, row_count * col_count)
    tile_ids = (lax.axis_index("rows") * row_count + lax.iota(jnp.int32, row_count)) // TILE
    support_mask = jnp.any(support[:, :, None] == tile_ids[None, None, :], axis=1).astype(
        jnp.float32
    )
    gram_part = jnp.dot(traces, traces.T, preferred_element_type=jnp.float32)
    all_flat = footprints.reshape(components, row_count * col_count)
    product = jnp.dot(traces, flattened, preferred_element_type=jnp.float32)
    gram_matrix, projected = lax.psum((gram_part, product), "tm")
    diagonal = jnp.diagonal(gram_matrix)
    stepped = descend(footprints, all_flat, gram_matrix, projected, diagonal, support_mask)
    result = spread(stepped, correlation) * support_mask[:, :, None]
    return result


def solution(mesh):
    return jax.shard_map(
        per_device,
        mesh=mesh,
        in_specs=(
            P("tm", ("band", "rows"), None),
            P("band", "tm"),
            P(None, ("band", "rows"), None),
            P(("band", "rows"), None),
            P("band", None),
        ),
        out_specs=P(None, ("band", "rows"), None),
        check_vma=False,
    )
```

profile of v0, /device:TPU:1, one launch (start us, length us, event | category | flops | bytes accessed | tf_op | source)
XLA Modules:
  0.0 112.9 jit_solution(9815881409470797042)
XLA Ops:
  6.5 0.0 copy-start
  6.5 0.0 all-reduce.6.cloned.1.call-start
  6.5 12.2 %copy.22 = bf16[128,8,8,512]{3,1,2,0:T(8,128)(2,1)} copy(bf16[128,8,8,512]{3,2,1,0:T(8,128)(2,1)} %bitcast.23) | data formatting | bytes 16777216
  18.8 0.0 copy-done
  18.8 0.0 copy-start.1
  18.8 6.0 %fusion.30 = f32[64,4096]{1,0:T(8,128)} fusion(bf16[64,1024]{1,0:T(8,128)(2,1)S(1)} %copy-done, bf16[1024,4096]{1,0:T(8,128)(2,1)} %bitcast.22), kind=kOutput, calls=%fused_computation.60 | convolution fusion | flops 536870912 | bytes 9568256 | tf_op jit(solution)/shard_map/dot_general | solution.py:70
  24.8 0.0 copy-start.3
  24.8 0.0 all-reduce.6.cloned.1.call-update
  24.8 0.0 copy-done.1
  24.8 0.6 copy.21
  25.4 0.0 copy-done.3
  25.5 0.1 compare_reduce_fusion
  25.5 0.1 copy.16
  25.6 0.2 fusion.29
  25.8 16.9 %psum.14 = f32[64,64]{1,0:T(8,128)S(1)} all-reduce(f32[64,64]{1,0:T(8,128)S(1)} %fusion.29), channel_id=1, replica_groups=mesh['band'=2,'tm'=4,'rows'=4] {'tm'}, use_global_device_ids=true, to_apply=%region_0.1 | all-reduce | flops 4096 | bytes 32768 | tf_op jit(solution)/shard_map/psum | solution.py:71
  42.7 0.8 gather_fusion
  43.5 36.2 %all-reduce.6.cloned.1.call-done = f32[64,4096]{1,0:T(8,128)} async-done(((f32[64,4096]{1,0:T(8,128)}), f32[64,4096]{1,0:T(8,128)}) %all-reduce.6.cloned.1.call-update) | async-done | bytes 1048592 | tf_op jit(solution)/shard_map/psum | solution.py:71
  79.8 2.4 %fusion.3 = f32[64,4096]{1,0:T(8,128)S(1)} fusion(f32[64,4096]{1,0:T(8,128)S(1)} %bitcast.25, f32[64,4096]{1,0:T(8,128)} %all-reduce.6.cloned.1.call-done, f32[64,64]{1,0:T(8,128)S(1)} %psum.14, f32[64]{0:T(128)S(1)} %broadcast_add_fusion), kind=kOutput, calls=%fused_computation.5 | convolution fusion | flops 202637312 | bytes 3162368 | tf_op jit(solution)/shard_map/dot_general | solution.py:48
  82.1 0.0 copy-start.2
  82.2 0.6 copy.23
  82.8 0.1 bitcast_multiply_fusion
  82.9 0.0 copy-done.2
  82.9 0.2 fusion.25
  83.1 0.2 copy.17
  83.3 3.5 %collective-permute-start = (f32[65,4,512]{2,0,1:T(8,128)S(1)}, f32[65,4,512]{2,0,1:T(8,128)S(1)}, u32[]{:S(2)}, u32[]{:S(2)}) collective-permute-start(f32[65,4,512]{2,0,1:T(8,128)S(1)} %copy.17), channel_id=1, source_target_pairs={{0,1},{1,2},{2,3},{4,5},{5,6},{6,7},{8,9},{9,10},{10,11},{12,13},{... | collective-permute-start | bytes 1597448 | tf_op jit(solution)/shard_map/ppermute | solution.py:20
  86.7 0.2 copy.18
  86.9 2.1 %collective-permute-start.1 = (f32[65,4,512]{2,0,1:T(8,128)S(1)}, f32[65,4,512]{2,0,1:T(8,128)S(1)}, u32[]{:S(2)}, u32[]{:S(2)}) collective-permute-start(f32[65,4,512]{2,0,1:T(8,128)S(1)} %copy.18), channel_id=1, source_target_pairs={{1,0},{2,1},{3,2},{5,4},{6,5},{7,6},{9,8},{10,9},{11,10},{13,12},{... | collective-permute-start | bytes 1597448 | tf_op jit(solution)/shard_map/ppermute | solution.py:23
  89.0 4.5 %collective-permute-done = f32[65,4,512]{2,0,1:T(8,128)S(1)} collective-permute-done((f32[65,4,512]{2,0,1:T(8,128)S(1)}, f32[65,4,512]{2,0,1:T(8,128)S(1)}, u32[]{:S(2)}, u32[]{:S(2)}) %collective-permute-start) | collective-permute-done | bytes 532512 | tf_op jit(solution)/shard_map/ppermute | solution.py:20
  93.5 0.3 copy.19
  93.9 4.2 %collective-permute-done.1 = f32[65,4,512]{2,0,1:T(8,128)S(1)} collective-permute-done((f32[65,4,512]{2,0,1:T(8,128)S(1)}, f32[65,4,512]{2,0,1:T(8,128)S(1)}, u32[]{:S(2)}, u32[]{:S(2)}) %collective-permute-start.1) | collective-permute-done | bytes 532512 | tf_op jit(solution)/shard_map/ppermute | solution.py:23
  98.1 0.3 copy.20
  98.5 0.4 pad_maximum_fusion
  98.9 0.4 slice.119
  99.3 1.3 %fusion.8 = f32[64,14,512]{2,1,0:T(8,128)S(1)} fusion(f32[64,14,512]{2,1,0:T(8,128)S(1)} %slice.119, f32[65,16,512]{2,1,0:T(8,128)S(1)} %pad_maximum_fusion, f32[14,512]{1,0:T(8,128)S(1)} %fusion.28), kind=kLoop, calls=%fused_computation.17 | loop fusion | flops 3211264 | bytes 7368704 | tf_op jit(solution)/shard_map/add | solution.py:31
  100.6 0.4 slice.122
  101.0 1.3 %fusion.13 = f32[64,12,512]{2,1,0:T(8,128)S(1)} fusion(f32[64,12,512]{2,1,0:T(8,128)S(1)} %slice.122, f32[64,14,512]{2,1,0:T(8,128)S(1)} %fusion.8, f32[12,512]{1,0:T(8,128)S(1)} %fusion.27), kind=kLoop, calls=%fused_computation.22 | loop fusion | flops 2752512 | bytes 6316032 | tf_op jit(solution)/shard_map/add | solution.py:31
  102.3 0.4 slice.125
  102.7 1.3 %fusion.18 = f32[64,10,512]{2,1,0:T(8,128)S(1)} fusion(f32[64,10,512]{2,1,0:T(8,128)S(1)} %slice.125, f32[64,12,512]{2,1,0:T(8,128)S(1)} %fusion.13, f32[10,512]{1,0:T(8,128)S(1)} %fusion.26), kind=kLoop, calls=%fused_computation.27 | loop fusion | flops 2293760 | bytes 5263360 | tf_op jit(solution)/shard_map/add | solution.py:31
  104.0 0.2 slice.128
  104.2 1.8 %fusion.24 = f32[64,8,512]{2,1,0:T(8,128)} fusion(f32[64,8,512]{2,1,0:T(8,128)S(1)} %slice.128, f32[64,10,512]{2,1,0:T(8,128)S(1)} %fusion.18, f32[8,512]{1,0:T(8,128)S(1)} %broadcast_multiply_fusion, f32[64,8]{1,0:T(8,128)S(1)} %copy.16), kind=kLoop, calls=%fused_computation.40 | loop fusion | flops 2097152 | bytes 4212736 | tf_op jit(solution)/shard_map/mul | solution.py:74
  (8 shorter events, 0.1 us)
Async XLA Ops:
  6.5 12.2 %copy-start = (bf16[64,1024]{1,0:T(8,128)(2,1)S(1)}, bf16[64,1024]{1,0:T(8,128)(2,1)}, u32[]{:S(2)}) copy-start(bf16[64,1024]{1,0:T(8,128)(2,1)} %param.6) | copy-start | bytes 393220
  6.5 73.2 %all-reduce.6.cloned.1.call-start = ((), (), s32[]{:S(2)}) async-start(), calls=%async_computation | async-start | bytes 2097152 | tf_op jit(solution)/shard_map/psum | solution.py:71
  18.8 6.0 %copy-start.1 = (f32[64,8,512]{2,1,0:T(8,128)S(1)}, f32[64,8,512]{2,1,0:T(8,128)}, u32[]{:S(2)}) copy-start(f32[64,8,512]{2,1,0:T(8,128)} %param.7) | copy-start | bytes 3145732
  24.8 0.7 copy-start.3
  82.1 0.8 copy-start.2
  83.3 10.3 %collective-permute-start = (f32[65,4,512]{2,0,1:T(8,128)S(1)}, f32[65,4,512]{2,0,1:T(8,128)S(1)}, u32[]{:S(2)}, u32[]{:S(2)}) collective-permute-start(f32[65,4,512]{2,0,1:T(8,128)S(1)} %copy.17), channel_id=1, source_target_pairs={{0,1},{1,2},{2,3},{4,5},{5,6},{6,7},{8,9},{9,10},{10,11},{12,13},{... | collective-permute-start | bytes 1597448 | tf_op jit(solution)/shard_map/ppermute | solution.py:20
  86.9 11.2 %collective-permute-start.1 = (f32[65,4,512]{2,0,1:T(8,128)S(1)}, f32[65,4,512]{2,0,1:T(8,128)S(1)}, u32[]{:S(2)}, u32[]{:S(2)}) collective-permute-start(f32[65,4,512]{2,0,1:T(8,128)S(1)} %copy.18), channel_id=1, source_target_pairs={{1,0},{2,1},{3,2},{5,4},{6,5},{7,6},{9,8},{10,9},{11,10},{13,12},{... | collective-permute-start | bytes 1597448 | tf_op jit(solution)/shard_map/ppermute | solution.py:23
Sparse Core Ops, SparseCore 0:
  24.9 54.8 all-reduce.5
where the time goes:
time: 113 us
  waiting for transfers between devices  45 us (40%)
  blocking collectives  16.9 us (15%)
  local copies, waits for them, and re-layouts  16.7 us (15%)
  between operations  13.6 us (12%)
  matrix products  8.54 us (8%)
  other arithmetic  6.57 us (6%)
  starting transfers between devices  5.55 us (5%)
    psum x1, waiting for transfers between devices, per_device(): gram_matrix, projected = lax.psum((gram_part, product), 'tm')  36.2 us
    psum x1, blocking collectives, per_device(): gram_matrix, projected = lax.psum((gram_part, product), 'tm')  16.9 us
    unnamed x11, local copies, waits for them, and re-layouts  13.5 us
    dot_general x1, matrix products, per_device(): product = jnp.dot(traces, flattened, preferred_element_type=jnp.float32)  6.01 us
    ppermute x1, waiting for transfers between devices, extended_2(): lax.ppermute(lax.slice_in_dim(block, block.shape[dim] - width, None, axis...  4.5 us
    ppermute x1, waiting for transfers between devices, extended_2(): lax.ppermute(lax.slice_in_dim(block, 0, width, axis=dim), axis, backward)  4.23 us
    add x3, other arithmetic, relax_once(): return center + diffusion_rate * weight * (beside_all - 4.0 * center)  3.95 us
    ppermute x1, starting transfers between devices, extended_2(): lax.ppermute(lax.slice_in_dim(block, block.shape[dim] - width, None, axis...  3.45 us
  transfers between devices with their start and end apart: 3, of which 3 were waited for; matrix products, arithmetic and copies ran while one was open for 2% of the time, Pallas kernels for 0%

commit v1 on v0

v1 whole, which is shorter than its diff:
```python
import jax
import jax.numpy as jnp
from jax import lax
from jax.sharding import PartitionSpec as P
from jax.experimental import pallas as pl
from jax.experimental.pallas import tpu as pltpu

TILE = 4
PASSES = 4
diffusion_rate = 0.24
step_scale = 0.5
epsilon = 1e-06
TIME_BLOCK = 256
LANES = 128
HIGHEST = lax.Precision.HIGHEST


def barrier(*arrays):
    return lax.optimization_barrier(arrays)


def project_kernel(traces_ref, movie_ref, *refs):
    *out_refs, spread_ref, wide_ref, total_ref, gram_ref = refs
    comps, frames = traces_ref.shape
    rows = movie_ref.shape[0] // frames
    step = pl.program_id(0)

    @pl.when(step == 0)
    def _():
        frame = lax.broadcasted_iota(jnp.int32, spread_ref.shape, 0)
        lane = lax.broadcasted_iota(jnp.int32, spread_ref.shape, 1)
        spread_ref[...] = jnp.where(frame == lane // rows, 1.0, 0.0).astype(jnp.bfloat16)

    traces = traces_ref[...]
    repeated = jnp.dot(traces, spread_ref[...], preferred_element_type=jnp.float32).astype(jnp.bfloat16)
    phase = lax.broadcasted_iota(jnp.int32, repeated.shape, 1) % rows
    for row in range(rows):
        wide_ref[row * comps : (row + 1) * comps, :] = jnp.where(
            phase == row, repeated, jnp.zeros_like(repeated)
        )
    part = jnp.dot(wide_ref[...], movie_ref[...], preferred_element_type=jnp.float32)
    gram = lax.dot_general(traces, traces, (((1,), (1,)), ((), ())), preferred_element_type=jnp.float32)

    @pl.when(step == 0)
    def _():
        total_ref[...] = part
        gram_ref[...] = gram

    @pl.when(step > 0)
    def _():
        total_ref[...] += part
        gram_ref[...] += gram

    @pl.when(step == pl.num_programs(0) - 1)
    def _():
        for row in range(rows):
            out_refs[row][0:comps, :] = total_ref[row * comps : (row + 1) * comps, :]
        band = comps * LANES // movie_ref.shape[1] // 2
        for half in range(2):
            ref = out_refs[half]
            ref[comps:, :] = jnp.zeros((band, ref.shape[1]), jnp.float32)
            for part_index in range(ref.shape[1] // LANES):
                first = (2 * part_index + half) * band
                ref[comps:, part_index * LANES : part_index * LANES + comps] = gram_ref[first : first + band, :]


def project(traces, recording):
    frames, rows, cols = recording.shape
    comps = traces.shape[0]
    band = comps * LANES // cols // 2
    heights = [comps + (band if row < 2 else 0) for row in range(rows)]
    return pl.pallas_call(
        project_kernel,
        name="project",
        grid=(frames // TIME_BLOCK,),
        in_specs=[
            pl.BlockSpec((comps, TIME_BLOCK), lambda i: (0, i)),
            pl.BlockSpec((TIME_BLOCK * rows, cols), lambda i: (i, 0)),
        ],
        out_specs=[pl.BlockSpec((height, cols), lambda i: (0, 0)) for height in heights],
        out_shape=[jax.ShapeDtypeStruct((height, cols), jnp.float32) for height in heights],
        scratch_shapes=[
            pltpu.VMEM((TIME_BLOCK, TIME_BLOCK * rows), jnp.bfloat16),
            pltpu.VMEM((rows * comps, TIME_BLOCK * rows), jnp.bfloat16),
            pltpu.VMEM((rows * comps, cols), jnp.float32),
            pltpu.VMEM((comps, comps), jnp.float32),
        ],
        compiler_params=pltpu.CompilerParams(
            vmem_limit_bytes=58 << 20, dimension_semantics=("arbitrary",)
        ),
    )(traces, recording.reshape(frames * rows, cols))


def tiles_of(array):
    comps, rows, cols = array.shape
    pieces = array.reshape(comps, rows, cols // LANES, LANES).transpose(0, 2, 1, 3)
    return pieces.reshape(comps * rows * cols // LANES, LANES)


def from_tiles(tiles, comps, rows, cols):
    pieces = tiles.reshape(comps, cols // LANES, rows, LANES).transpose(0, 2, 1, 3)
    return pieces.reshape(comps, rows, cols)


def descend_kernel(where_ref, support_ref, footprints_ref, *refs):
    *sum_refs, out_ref = refs
    comps, cols = out_ref.shape[1:]
    rows = out_ref.shape[0]
    swapped = where_ref[1] == 1
    band = sum_refs[0].shape[0] - comps
    pairs = [
        tuple(
            jnp.where(swapped, sum_refs[2 * chunk + 1 - half][...], sum_refs[2 * chunk + half][...])
            for half in range(2)
        )
        for chunk in range(rows // 2)
    ]
    gram = jnp.concatenate(
        [
            pairs[0][half][comps:, part * LANES : part * LANES + comps]
            for part in range(cols // LANES)
            for half in range(2)
        ],
        axis=0,
    )
    own = lax.broadcasted_iota(jnp.int32, gram.shape, 0) == lax.broadcasted_iota(jnp.int32, gram.shape, 1)
    diagonal = jnp.sum(jnp.where(own, gram, 0.0), axis=1, keepdims=True)
    rate = step_scale / (diagonal + epsilon)
    for row in range(rows):
        tile = (where_ref[0] * rows + row) // TILE
        mask = jnp.max(jnp.where(support_ref[...] == tile, 1.0, 0.0), axis=1, keepdims=True)
        field = jnp.concatenate(
            [
                footprints_ref[pl.ds(piece * rows + row, comps, stride=rows * cols // LANES), :]
                for piece in range(cols // LANES)
            ],
            axis=1,
        )
        gradient = (
            jnp.dot(gram, field, precision=HIGHEST, preferred_element_type=jnp.float32)
            - pairs[row // 2][row % 2][0:comps]
        )
        out_ref[row] = jnp.maximum(field - rate * gradient, 0.0) * mask


def descend(where, support, footprints, sums):
    comps, rows, cols = footprints.shape
    return pl.pallas_call(
        descend_kernel,
        name="descend",
        in_specs=[pl.BlockSpec(memory_space=pltpu.SMEM)] + [pl.BlockSpec(memory_space=pltpu.VMEM)] * (2 + len(sums)),
        out_specs=pl.BlockSpec(memory_space=pltpu.VMEM),
        out_shape=jax.ShapeDtypeStruct((rows, comps, cols), jnp.float32),
        compiler_params=pltpu.CompilerParams(vmem_limit_bytes=40 << 20),
    )(where, support, tiles_of(footprints), *sums)


def diffuse_kernel(where_ref, support_ref, correlation_ref, field_ref, inner_ref, outer_ref, out_ref):
    rows, group, cols = field_ref.shape
    index, last = where_ref[0], where_ref[2]
    even = index % 2 == 0
    has_above = jnp.where(index > 0, 1.0, 0.0)
    has_below = jnp.where(index < last, 1.0, 0.0)
    planes = [
        jnp.where(even, outer_ref[row], inner_ref[row]) * has_above for row in range(PASSES)
    ]
    planes += [field_ref[row] for row in range(rows)]
    planes += [
        jnp.where(even, inner_ref[row], outer_ref[row]) * has_below for row in range(PASSES)
    ]
    lane = lax.broadcasted_iota(jnp.int32, (group, cols), 1)
    for pass_index in range(PASSES):
        renewed = []
        for row in range(1, len(planes) - 1):
            center = planes[row]
            left = jnp.where(lane == 0, 0.0, pltpu.roll(center, 1, 1))
            right = jnp.where(lane == cols - 1, 0.0, pltpu.roll(center, cols - 1, 1))
            weight = diffusion_rate * correlation_ref[row + pass_index : row + pass_index + 1, :]
            beside = planes[row - 1] + planes[row + 1] + left + right
            renewed.append(center + weight * (beside - 4.0 * center))
        planes = renewed
    for row in range(rows):
        tile = (index * rows + row) // TILE
        mask = jnp.max(jnp.where(support_ref[...] == tile, 1.0, 0.0), axis=1, keepdims=True)
        masked = planes[row] * mask
        for piece in range(cols // LANES):
            out_ref[pl.ds(piece * rows + row, group, stride=rows * cols // LANES), :] = masked[
                :, piece * LANES : (piece + 1) * LANES
            ]


def diffuse(where, support, correlation, field, inner, outer):
    rows, comps, cols = field.shape
    group = 8
    return pl.pallas_call(
        diffuse_kernel,
        name="diffuse",
        grid=(comps // group,),
        in_specs=[
            pl.BlockSpec(memory_space=pltpu.SMEM),
            pl.BlockSpec((group, support.shape[1]), lambda i: (i, 0)),
            pl.BlockSpec(correlation.shape, lambda i: (0, 0)),
            pl.BlockSpec((rows, group, cols), lambda i: (0, i, 0)),
            pl.BlockSpec((PASSES, group, cols), lambda i: (0, i, 0)),
            pl.BlockSpec((PASSES, group, cols), lambda i: (0, i, 0)),
        ],
        out_specs=pl.BlockSpec((group * rows * cols // LANES, LANES), lambda i: (i, 0)),
        out_shape=jax.ShapeDtypeStruct((comps * rows * cols // LANES, LANES), jnp.float32),
        compiler_params=pltpu.CompilerParams(
            vmem_limit_bytes=40 << 20, dimension_semantics=("arbitrary",)
        ),
    )(where, support, correlation, field, inner, outer)


def pairs_of(count, first):
    table = list(range(count))
    for i in range(first, count - 1, 2):
        table[i], table[i + 1] = i + 1, i
    return list(enumerate(table))


def total_over_frames(parts, odd):
    count = lax.axis_size("tm")
    sums = []
    if count != 4:
        for low, high in zip(parts[::2], parts[1::2]):
            low, high = lax.psum((low, high), "tm")
            sums += [jnp.where(odd, high, low), jnp.where(odd, low, high)]
        return sums
    near, far = pairs_of(4, 0), [(0, 3), (1, 2), (2, 1), (3, 0)]
    firsts = []
    for low, high in zip(parts[::2], parts[1::2]):
        mine, other = barrier(jnp.where(odd, high, low), jnp.where(odd, low, high))
        firsts.append((mine, lax.ppermute(other, "tm", near)))
    for mine, received in firsts:
        (received,) = barrier(received)
        (half,) = barrier(mine + received)
        (across,) = barrier(lax.ppermute(half, "tm", far))
        (whole,) = barrier(half + across)
        sums += [whole, lax.ppermute(whole, "tm", near)]
    return sums


def per_device(recording, traces, footprints, correlation, support):
    comps, rows, cols = footprints.shape
    index = lax.axis_index("rows")
    count = lax.axis_size("rows")
    part = lax.axis_index("tm")
    odd = (part == 1) | (part == 2)
    where = jnp.stack([index, odd.astype(jnp.int32), jnp.int32(count - 1)]).astype(jnp.int32)
    inside, outside = pairs_of(count, 0), pairs_of(count, 1)
    even = index % 2 == 0

    near = lax.ppermute(correlation, "rows", inside)
    away = lax.ppermute(correlation, "rows", outside)
    above, below = jnp.where(even, away, near), jnp.where(even, near, away)
    above = jnp.where(index > 0, above[rows - PASSES :], 0.0)
    below = jnp.where(index < count - 1, below[:PASSES], 0.0)
    weights = jnp.concatenate([above, correlation, below], axis=0)

    parts = project(traces, recording)
    sums = total_over_frames(parts, odd)
    stepped = descend(where, support, footprints, sums)
    top, bottom = stepped[:PASSES], stepped[rows - PASSES :]
    to_inner, to_outer = barrier(jnp.where(even, bottom, top), jnp.where(even, top, bottom))
    inner = lax.ppermute(to_inner, "rows", inside)
    outer = lax.ppermute(to_outer, "rows", outside)
    result = diffuse(where, support, weights, stepped, inner, outer)
    return from_tiles(result, comps, rows, cols)


def solution(mesh):
    return jax.shard_map(
        per_device,
        mesh=mesh,
        in_specs=(
            P("tm", ("band", "rows"), None),
            P("band", "tm"),
            P(None, ("band", "rows"), None),
            P(("band", "rows"), None),
            P("band", None),
        ),
        out_specs=P(None, ("band", "rows"), None),
        check_vma=False,
    )
```

time: 113 us -> 71 us (0.63)
  waiting for transfers between devices: 45 us -> 16.4 us
  starting transfers between devices: 5.55 us -> 32.6 us
  Pallas kernels: 0 us -> 17.2 us
  blocking collectives: 16.9 us -> 0 us
  local copies, waits for them, and re-layouts: 16.7 us -> 0.11 us
  between operations: 13.6 us -> 0.15 us
  matrix products: 8.54 us -> 0 us
  other arithmetic: 6.57 us -> 4.32 us
    psum x1 -> x0, waiting for transfers between devices: 36.2 us -> none  [per_device(): gram_matrix, projected = lax.psum((gram_part, product), 'tm')]
    ppermute x2 -> x16, starting transfers between devices: 5.55 us -> 32.6 us  [the longest x4 11.5 us: total_over_frames(): across, = barrier(lax.ppermute(half, 'tm', far))]
    pallas_call x0 -> x3, Pallas kernels: none -> 17.2 us  [the longest x1 9.11 us: project(): pl.pallas_call(project_kernel, name='project', grid=(frames // TIME_BLOCK...]
    psum x1 -> x0, blocking collectives: 16.9 us -> none  [per_device(): gram_matrix, projected = lax.psum((gram_part, product), 'tm')]
    unnamed x11 -> x7, local copies, waits for them, and re-layouts: 13.5 us -> 0.11 us
    dot_general x3 -> x0, matrix products: 8.54 us -> none  [the longest x1 6.01 us: per_device(): product = jnp.dot(traces, flattened, preferred_element_type=jnp.float32)]
    ppermute x2 -> x16, waiting for transfers between devices: 8.73 us -> 16.4 us  [the longest x4 7.4 us: total_over_frames(): across, = barrier(lax.ppermute(half, 'tm', far))]
    select_n x1 -> x5, other arithmetic: 0.01 us -> 4.07 us  [the longest x3 3.12 us: total_over_frames(): mine, other = barrier(jnp.where(odd, high, low), jnp.where(odd, low, high))]
  transfers between devices with their start and end apart: 3 -> 16, of which waited for: 3 -> 6; matrix products, arithmetic and copies ran while one was open for 2% -> 3% of each run, Pallas kernels for 0% -> 0%
where the time goes in v1:
time: 71 us; the launch traced here: 70.8 us
  starting transfers between devices  32.6 us (46%)
  Pallas kernels  17.2 us (24%)
  waiting for transfers between devices  16.4 us (23%)
  other arithmetic  4.32 us (6%)
    ppermute x4, starting transfers between devices, total_over_frames(): across, = barrier(lax.ppermute(half, 'tm', far))  11.5 us
    pallas_call x1, Pallas kernels, project(): pl.pallas_call(project_kernel, name='project', grid=(frames // TIME_BLOCK...  9.11 us
    ppermute x4, starting transfers between devices, total_over_frames(): sums += [whole, lax.ppermute(whole, 'tm', near)]  7.67 us
    ppermute x4, waiting for transfers between devices, total_over_frames(): across, = barrier(lax.ppermute(half, 'tm', far))  7.4 us
    pallas_call x1, Pallas kernels, diffuse(): pl.pallas_call(diffuse_kernel, name='diffuse', grid=(comps // group,), in...  6.18 us
    ppermute x1, waiting for transfers between devices, per_device(): away = lax.ppermute(correlation, 'rows', outside)  5 us
    ppermute x1, starting transfers between devices, per_device(): inner = lax.ppermute(to_inner, 'rows', inside)  3.93 us
    ppermute x4, waiting for transfers between devices, total_over_frames(): sums += [whole, lax.ppermute(whole, 'tm', near)]  3.93 us
  transfers between devices with their start and end apart: 16, of which 6 were waited for; matrix products, arithmetic and copies ran while one was open for 3% of the time, Pallas kernels for 0%

profile of v1, /device:TPU:1, one launch (start us, length us, event | category | flops | bytes accessed | tf_op | source)
XLA Modules:
  0.0 70.8 jit_solution(879649524752704161)
XLA Ops:
  0.0 0.0 copy-start.2
  0.0 0.0 copy-start
  0.0 0.0 copy-start.1
  0.0 9.1 %project.1 = (f32[72,512]{1,0:T(8,128)}, f32[72,512]{1,0:T(8,128)}, f32[64,512]{1,0:T(8,128)}, f32[64,512]{1,0:T(8,128)}, f32[64,512]{1,0:T(8,128)}, /*index=5*/...) custom-call(bf16[64,1024]{1,0:T(8,128)(2,1)} %traces_ref.1, bf16[8192,512]{1,0:T(8,128)(2,1)} %bitcast.14), custom_call_target="tpu_custom_call" | custom-call | tf_op jit(solution)/shard_map/project/pallas_call | solution.py:72
  9.1 1.0 %broadcast_select_fusion = (f32[72,512]{1,0:T(8,128)S(1)}, f32[72,512]{1,0:T(8,128)S(1)}) fusion(f32[72,512]{1,0:T(8,128)} %get-tuple-element.24, f32[72,512]{1,0:T(8,128)} %get-tuple-element.23, pred[]{:T(512)S(6)} %or.3), kind=kLoop, calls=%fused_computation.2 | loop fusion | flops 73728 | bytes 589825 | tf_op jit(solution)/shard_map/jit(_where)/select_n | solution.py:233
  10.1 2.2 %collective-permute-start.2 = (f32[72,512]{1,0:T(8,128)S(1)}, f32[72,512]{1,0:T(8,128)S(1)}, u32[]{:S(2)}, u32[]{:S(2)}) collective-permute-start(f32[72,512]{1,0:T(8,128)S(1)} %get-tuple-element.26), channel_id=1, source_target_pairs={{0,4},{4,0},{8,12},{12,8},{1,5},{5,1},{9,13},{13,9},{2,6},{6,2},{1... | collective-permute-start | bytes 442376 | tf_op jit(solution)/shard_map/ppermute | solution.py:234
  12.3 1.1 %broadcast_select_fusion.2 = (f32[64,512]{1,0:T(8,128)S(1)}, f32[64,512]{1,0:T(8,128)S(1)}, f32[64,512]{1,0:T(8,128)S(1)}, f32[64,512]{1,0:T(8,128)S(1)}) fusion(f32[64,512]{1,0:T(8,128)} %get-tuple-element.36, f32[64,512]{1,0:T(8,128)} %get-tuple-element.35, pred[]{:T(512)S(6)} %or.3, f32[64,512]{1,0:T(8,128)} %get-tuple-element.31, ...), kind=kLoop, calls=%fused_computation.4 | loop fusion | flops 131072 | bytes 1048577 | tf_op jit(solution)/shard_map/jit(_where)/select_n | solution.py:233
  13.4 0.1 collective-permute-start.8
  13.5 1.4 %collective-permute-start.11 = (f32[64,512]{1,0:T(8,128)S(1)}, f32[64,512]{1,0:T(8,128)S(1)}, u32[]{:S(2)}, u32[]{:S(2)}) collective-permute-start(f32[64,512]{1,0:T(8,128)S(1)} %get-tuple-element.38), channel_id=1, source_target_pairs={{0,4},{4,0},{8,12},{12,8},{1,5},{5,1},{9,13},{13,9},{2,6},{6,2},{1... | collective-permute-start | bytes 393224 | tf_op jit(solution)/shard_map/ppermute | solution.py:234
  15.0 1.0 %broadcast_select_fusion.6 = (f32[64,512]{1,0:T(8,128)S(1)}, f32[64,512]{1,0:T(8,128)S(1)}) fusion(f32[64,512]{1,0:T(8,128)} %get-tuple-element.28, f32[64,512]{1,0:T(8,128)} %get-tuple-element.27, pred[]{:T(512)S(6)} %or.3), kind=kLoop, calls=%fused_computation.8 | loop fusion | flops 65536 | bytes 524289 | tf_op jit(solution)/shard_map/jit(_where)/select_n | solution.py:233
  16.0 0.2 collective-permute-start.5
  16.1 0.0 collective-permute-done.2
  16.2 3.5 %collective-permute-start.3 = (f32[72,512]{1,0:T(8,128)S(1)}, f32[72,512]{1,0:T(8,128)S(1)}, u32[]{:S(2)}, u32[]{:S(2)}) collective-permute-start(f32[72,512]{1,0:T(8,128)S(1)} %add.29), channel_id=1, source_target_pairs={{0,12},{4,8},{8,4},{12,0},{1,13},{5,9},{9,5},{13,1},{2,14},{6,10},... | collective-permute-start | bytes 442376 | tf_op jit(solution)/shard_map/ppermute | solution.py:238
  19.6 0.0 collective-permute-done.8
  19.6 2.3 %collective-permute-start.9 = (f32[64,512]{1,0:T(8,128)S(1)}, f32[64,512]{1,0:T(8,128)S(1)}, u32[]{:S(2)}, u32[]{:S(2)}) collective-permute-start(f32[64,512]{1,0:T(8,128)S(1)} %add.33), channel_id=1, source_target_pairs={{0,12},{4,8},{8,4},{12,0},{1,13},{5,9},{9,5},{13,1},{2,14},{6,10},... | collective-permute-start | bytes 393224 | tf_op jit(solution)/shard_map/ppermute | solution.py:238
  22.0 0.0 collective-permute-done.11
  22.0 2.8 %collective-permute-start.12 = (f32[64,512]{1,0:T(8,128)S(1)}, f32[64,512]{1,0:T(8,128)S(1)}, u32[]{:S(2)}, u32[]{:S(2)}) collective-permute-start(f32[64,512]{1,0:T(8,128)S(1)} %add.35), channel_id=1, source_target_pairs={{0,12},{4,8},{8,4},{12,0},{1,13},{5,9},{9,5},{13,1},{2,14},{6,10},... | collective-permute-start | bytes 393224 | tf_op jit(solution)/shard_map/ppermute | solution.py:238
  24.8 0.0 collective-permute-done.5
  24.8 3.0 %collective-permute-start.6 = (f32[64,512]{1,0:T(8,128)S(1)}, f32[64,512]{1,0:T(8,128)S(1)}, u32[]{:S(2)}, u32[]{:S(2)}) collective-permute-start(f32[64,512]{1,0:T(8,128)S(1)} %add.31), channel_id=1, source_target_pairs={{0,12},{4,8},{8,4},{12,0},{1,13},{5,9},{9,5},{13,1},{2,14},{6,10},... | collective-permute-start | bytes 393224 | tf_op jit(solution)/shard_map/ppermute | solution.py:238
  27.8 1.9 %collective-permute-done.3 = f32[72,512]{1,0:T(8,128)S(1)} collective-permute-done((f32[72,512]{1,0:T(8,128)S(1)}, f32[72,512]{1,0:T(8,128)S(1)}, u32[]{:S(2)}, u32[]{:S(2)}) %collective-permute-start.3) | collective-permute-done | bytes 147488 | tf_op jit(solution)/shard_map/ppermute | solution.py:238
  29.8 0.1 collective-permute-start.4
  29.8 2.7 %collective-permute-done.9 = f32[64,512]{1,0:T(8,128)S(1)} collective-permute-done((f32[64,512]{1,0:T(8,128)S(1)}, f32[64,512]{1,0:T(8,128)S(1)}, u32[]{:S(2)}, u32[]{:S(2)}) %collective-permute-start.9) | collective-permute-done | bytes 131104 | tf_op jit(solution)/shard_map/ppermute | solution.py:238
  32.6 0.1 collective-permute-start.10
  32.6 2.7 %collective-permute-done.12 = f32[64,512]{1,0:T(8,128)S(1)} collective-permute-done((f32[64,512]{1,0:T(8,128)S(1)}, f32[64,512]{1,0:T(8,128)S(1)}, u32[]{:S(2)}, u32[]{:S(2)}) %collective-permute-start.12) | collective-permute-done | bytes 131104 | tf_op jit(solution)/shard_map/ppermute | solution.py:238
  35.4 3.3 %collective-permute-start.13 = (f32[64,512]{1,0:T(8,128)S(1)}, f32[64,512]{1,0:T(8,128)S(1)}, u32[]{:S(2)}, u32[]{:S(2)}) collective-permute-start(f32[64,512]{1,0:T(8,128)S(1)} %add.36.refs_6_), channel_id=1, source_target_pairs={{0,4},{4,0},{8,12},{12,8},{1,5},{5,1},{9,13},{13,9},{2,6},{6,2},{1... | collective-permute-start | bytes 393224 | tf_op jit(solution)/shard_map/ppermute | solution.py:240
  38.8 0.0 collective-permute-done.6
  38.8 4.2 %collective-permute-start.7 = (f32[64,512]{1,0:T(8,128)S(1)}, f32[64,512]{1,0:T(8,128)S(1)}, u32[]{:S(2)}, u32[]{:S(2)}) collective-permute-start(f32[64,512]{1,0:T(8,128)S(1)} %add.32.refs_2_), channel_id=1, source_target_pairs={{0,4},{4,0},{8,12},{12,8},{1,5},{5,1},{9,13},{13,9},{2,6},{6,2},{1... | collective-permute-start | bytes 393224 | tf_op jit(solution)/shard_map/ppermute | solution.py:240
  43.0 0.0 copy-done.2
  43.0 0.1 copy.7.support_ref
  43.1 0.1 pad_add_fusion.where_ref
  43.1 0.0 collective-permute-done.10.refs_5_
  43.2 0.8 %collective-permute-done.13.refs_7_ = f32[64,512]{1,0:T(8,128)S(1)} collective-permute-done((f32[64,512]{1,0:T(8,128)S(1)}, f32[64,512]{1,0:T(8,128)S(1)}, u32[]{:S(2)}, u32[]{:S(2)}) %collective-permute-start.13) | collective-permute-done | bytes 131104 | tf_op jit(solution)/shard_map/ppermute | solution.py:240
  43.9 3.2 %collective-permute-done.7.refs_3_ = f32[64,512]{1,0:T(8,128)S(1)} collective-permute-done((f32[64,512]{1,0:T(8,128)S(1)}, f32[64,512]{1,0:T(8,128)S(1)}, u32[]{:S(2)}, u32[]{:S(2)}) %collective-permute-start.7) | collective-permute-done | bytes 131104 | tf_op jit(solution)/shard_map/ppermute | solution.py:240
  47.1 0.0 collective-permute-done.4.refs_1_
  47.1 0.0 copy-done
  47.1 1.9 %descend.1.field_ref = f32[8,64,512]{2,1,0:T(8,128)S(1)} custom-call(s32[3]{0:T(128)S(1)} %pad_add_fusion.where_ref, s32[64,4]{1,0:T(8,128)S(1)} %copy.7.support_ref, f32[2048,128]{1,0:T(8,128)S(1)} %bitcast.13, f32[72,512]{1,0:T(8,128)S(1)} %add.30.refs_0_, f32[72,512]{1,0:T(8,128)S(1)} %collective-permute-done.4.refs_1_, f32[64,512]{1,0:T(8,128)S(1)} %add.32.refs_2_, ...), custom_call_target="tpu_custom_call" | custom-call | tf_op jit(solution)/shard_map/descend/pallas_call | solution.py:148
  49.0 0.9 %slice_select_fusion = (f32[4,64,512]{2,1,0:T(8,128)S(1)}, f32[4,64,512]{2,1,0:T(8,128)}) fusion(f32[8,64,512]{2,1,0:T(8,128)S(1)} %descend.1.field_ref, pred[]{:T(512)S(6)} %eq.13), kind=kLoop, calls=%fused_computation | loop fusion | flops 262144 | bytes 2097153 | tf_op jit(solution)/shard_map/jit(_where)/select_n | solution.py:265
  49.9 3.9 %collective-permute-start.14 = (f32[4,64,512]{2,1,0:T(8,128)}, f32[4,64,512]{2,1,0:T(8,128)S(1)}, u32[]{:S(2)}, u32[]{:S(2)}) collective-permute-start(f32[4,64,512]{2,1,0:T(8,128)} %get-tuple-element.39), channel_id=1, source_target_pairs={{0,1},{1,0},{2,3},{3,2},{4,5},{5,4},{6,7},{7,6},{8,9},{9,8},{10,11... | collective-permute-start | bytes 1572872 | tf_op jit(solution)/shard_map/ppermute | solution.py:266
  53.9 3.0 %collective-permute-start.15 = (f32[4,64,512]{2,1,0:T(8,128)S(1)}, f32[4,64,512]{2,1,0:T(8,128)S(1)}, u32[]{:S(2)}, u32[]{:S(2)}) collective-permute-start(f32[4,64,512]{2,1,0:T(8,128)S(1)} %get-tuple-element.40), channel_id=1, source_target_pairs={{0,0},{1,2},{2,1},{3,3},{4,4},{5,6},{6,5},{7,7},{8,8},{9,10},{10,9... | collective-permute-start | bytes 1572872 | tf_op jit(solution)/shard_map/ppermute | solution.py:267
  56.9 0.0 copy-done.1
  56.9 2.6 %collective-permute-start = (f32[8,512]{1,0:T(8,128)S(1)}, f32[8,512]{1,0:T(8,128)S(1)}, u32[]{:S(2)}, u32[]{:S(2)}) collective-permute-start(f32[8,512]{1,0:T(8,128)S(1)} %copy-done.1), channel_id=1, source_target_pairs={{0,0},{1,2},{2,1},{3,3},{4,4},{5,6},{6,5},{7,7},{8,8},{9,10},{10,9... | collective-permute-start | bytes 49160 | tf_op jit(solution)/shard_map/ppermute | solution.py:255
  59.5 0.1 collective-permute-start.1
  59.5 5.0 %collective-permute-done = f32[8,512]{1,0:T(8,128)S(1)} collective-permute-done((f32[8,512]{1,0:T(8,128)S(1)}, f32[8,512]{1,0:T(8,128)S(1)}, u32[]{:S(2)}, u32[]{:S(2)}) %collective-permute-start) | collective-permute-done | bytes 16416 | tf_op jit(solution)/shard_map/ppermute | solution.py:255
  64.5 0.0 collective-permute-done.1
  64.6 0.0 collective-permute-done.14.inner_ref
  64.6 0.0 collective-permute-done.15.outer_ref
  64.6 6.2 %diffuse.1 = f32[2048,128]{1,0:T(8,128)} custom-call(s32[3]{0:T(128)S(1)} %pad_add_fusion.where_ref, s32[64,4]{1,0:T(8,128)S(1)} %copy.7.support_ref, f32[16,512]{1,0:T(8,128)S(1)} %pad_maximum_fusion.correlation_ref, f32[8,64,512]{2,1,0:T(8,128)S(1)} %descend.1.field_ref, f32[4,64,512]{2,1,0:T(8,128)S(1)} %collective-permute-done.14.inner_ref, ...), custom_call_target="tpu_custom_call" | custom-call | tf_op jit(solution)/shard_map/diffuse/pallas_call | solution.py:195
  (10 shorter events, 0.2 us)
Async XLA Ops:
  0.0 43.0 %copy-start.2 = (s32[64,4]{0,1:T(4,128)S(1)}, s32[64,4]{0,1:T(4,128)}, u32[]{:S(2)}) copy-start(s32[64,4]{0,1:T(4,128)} %param.9) | copy-start | bytes 3076
  0.0 47.1 %copy-start = (f32[64,8,512]{2,1,0:T(8,128)S(1)}, f32[64,8,512]{2,1,0:T(8,128)}, u32[]{:S(2)}) copy-start(f32[64,8,512]{2,1,0:T(8,128)} %param.7) | copy-start | bytes 3145732
  0.0 56.9 %copy-start.1 = (f32[8,512]{1,0:T(8,128)S(1)}, f32[8,512]{1,0:T(8,128)}, u32[]{:S(2)}) copy-start(f32[8,512]{1,0:T(8,128)} %param.8) | copy-start | bytes 49156
  10.1 6.0 %collective-permute-start.2 = (f32[72,512]{1,0:T(8,128)S(1)}, f32[72,512]{1,0:T(8,128)S(1)}, u32[]{:S(2)}, u32[]{:S(2)}) collective-permute-start(f32[72,512]{1,0:T(8,128)S(1)} %get-tuple-element.26), channel_id=1, source_target_pairs={{0,4},{4,0},{8,12},{12,8},{1,5},{5,1},{9,13},{13,9},{2,6},{6,2},{1... | collective-permute-start | bytes 442376 | tf_op jit(solution)/shard_map/ppermute | solution.py:234
  13.4 6.2 %collective-permute-start.8 = (f32[64,512]{1,0:T(8,128)S(1)}, f32[64,512]{1,0:T(8,128)S(1)}, u32[]{:S(2)}, u32[]{:S(2)}) collective-permute-start(f32[64,512]{1,0:T(8,128)S(1)} %get-tuple-element.34), channel_id=1, source_target_pairs={{0,4},{4,0},{8,12},{12,8},{1,5},{5,1},{9,13},{13,9},{2,6},{6,2},{1... | collective-permute-start | bytes 393224 | tf_op jit(solution)/shard_map/ppermute | solution.py:234
  13.5 8.4 %collective-permute-start.11 = (f32[64,512]{1,0:T(8,128)S(1)}, f32[64,512]{1,0:T(8,128)S(1)}, u32[]{:S(2)}, u32[]{:S(2)}) collective-permute-start(f32[64,512]{1,0:T(8,128)S(1)} %get-tuple-element.38), channel_id=1, source_target_pairs={{0,4},{4,0},{8,12},{12,8},{1,5},{5,1},{9,13},{13,9},{2,6},{6,2},{1... | collective-permute-start | bytes 393224 | tf_op jit(solution)/shard_map/ppermute | solution.py:234
  16.0 8.8 %collective-permute-start.5 = (f32[64,512]{1,0:T(8,128)S(1)}, f32[64,512]{1,0:T(8,128)S(1)}, u32[]{:S(2)}, u32[]{:S(2)}) collective-permute-start(f32[64,512]{1,0:T(8,128)S(1)} %get-tuple-element.30), channel_id=1, source_target_pairs={{0,4},{4,0},{8,12},{12,8},{1,5},{5,1},{9,13},{13,9},{2,6},{6,2},{1... | collective-permute-start | bytes 393224 | tf_op jit(solution)/shard_map/ppermute | solution.py:234
  16.2 13.6 %collective-permute-start.3 = (f32[72,512]{1,0:T(8,128)S(1)}, f32[72,512]{1,0:T(8,128)S(1)}, u32[]{:S(2)}, u32[]{:S(2)}) collective-permute-start(f32[72,512]{1,0:T(8,128)S(1)} %add.29), channel_id=1, source_target_pairs={{0,12},{4,8},{8,4},{12,0},{1,13},{5,9},{9,5},{13,1},{2,14},{6,10},... | collective-permute-start | bytes 442376 | tf_op jit(solution)/shard_map/ppermute | solution.py:238
  19.6 12.9 %collective-permute-start.9 = (f32[64,512]{1,0:T(8,128)S(1)}, f32[64,512]{1,0:T(8,128)S(1)}, u32[]{:S(2)}, u32[]{:S(2)}) collective-permute-start(f32[64,512]{1,0:T(8,128)S(1)} %add.33), channel_id=1, source_target_pairs={{0,12},{4,8},{8,4},{12,0},{1,13},{5,9},{9,5},{13,1},{2,14},{6,10},... | collective-permute-start | bytes 393224 | tf_op jit(solution)/shard_map/ppermute | solution.py:238
  22.0 13.4 %collective-permute-start.12 = (f32[64,512]{1,0:T(8,128)S(1)}, f32[64,512]{1,0:T(8,128)S(1)}, u32[]{:S(2)}, u32[]{:S(2)}) collective-permute-start(f32[64,512]{1,0:T(8,128)S(1)} %add.35), channel_id=1, source_target_pairs={{0,12},{4,8},{8,4},{12,0},{1,13},{5,9},{9,5},{13,1},{2,14},{6,10},... | collective-permute-start | bytes 393224 | tf_op jit(solution)/shard_map/ppermute | solution.py:238
  24.8 14.0 %collective-permute-start.6 = (f32[64,512]{1,0:T(8,128)S(1)}, f32[64,512]{1,0:T(8,128)S(1)}, u32[]{:S(2)}, u32[]{:S(2)}) collective-permute-start(f32[64,512]{1,0:T(8,128)S(1)} %add.31), channel_id=1, source_target_pairs={{0,12},{4,8},{8,4},{12,0},{1,13},{5,9},{9,5},{13,1},{2,14},{6,10},... | collective-permute-start | bytes 393224 | tf_op jit(solution)/shard_map/ppermute | solution.py:238
  29.8 17.3 %collective-permute-start.4 = (f32[72,512]{1,0:T(8,128)S(1)}, f32[72,512]{1,0:T(8,128)S(1)}, u32[]{:S(2)}, u32[]{:S(2)}) collective-permute-start(f32[72,512]{1,0:T(8,128)S(1)} %add.30.refs_0_), channel_id=1, source_target_pairs={{0,4},{4,0},{8,12},{12,8},{1,5},{5,1},{9,13},{13,9},{2,6},{6,2},{1... | collective-permute-start | bytes 442376 | tf_op jit(solution)/shard_map/ppermute | solution.py:240
  32.6 10.6 %collective-permute-start.10 = (f32[64,512]{1,0:T(8,128)S(1)}, f32[64,512]{1,0:T(8,128)S(1)}, u32[]{:S(2)}, u32[]{:S(2)}) collective-permute-start(f32[64,512]{1,0:T(8,128)S(1)} %add.34.refs_4_), channel_id=1, source_target_pairs={{0,4},{4,0},{8,12},{12,8},{1,5},{5,1},{9,13},{13,9},{2,6},{6,2},{1... | collective-permute-start | bytes 393224 | tf_op jit(solution)/shard_map/ppermute | solution.py:240
  35.4 8.5 %collective-permute-start.13 = (f32[64,512]{1,0:T(8,128)S(1)}, f32[64,512]{1,0:T(8,128)S(1)}, u32[]{:S(2)}, u32[]{:S(2)}) collective-permute-start(f32[64,512]{1,0:T(8,128)S(1)} %add.36.refs_6_), channel_id=1, source_target_pairs={{0,4},{4,0},{8,12},{12,8},{1,5},{5,1},{9,13},{13,9},{2,6},{6,2},{1... | collective-permute-start | bytes 393224 | tf_op jit(solution)/shard_map/ppermute | solution.py:240
  38.8 8.3 %collective-permute-start.7 = (f32[64,512]{1,0:T(8,128)S(1)}, f32[64,512]{1,0:T(8,128)S(1)}, u32[]{:S(2)}, u32[]{:S(2)}) collective-permute-start(f32[64,512]{1,0:T(8,128)S(1)} %add.32.refs_2_), channel_id=1, source_target_pairs={{0,4},{4,0},{8,12},{12,8},{1,5},{5,1},{9,13},{13,9},{2,6},{6,2},{1... | collective-permute-start | bytes 393224 | tf_op jit(solution)/shard_map/ppermute | solution.py:240
  49.9 14.6 %collective-permute-start.14 = (f32[4,64,512]{2,1,0:T(8,128)}, f32[4,64,512]{2,1,0:T(8,128)S(1)}, u32[]{:S(2)}, u32[]{:S(2)}) collective-permute-start(f32[4,64,512]{2,1,0:T(8,128)} %get-tuple-element.39), channel_id=1, source_target_pairs={{0,1},{1,0},{2,3},{3,2},{4,5},{5,4},{6,7},{7,6},{8,9},{9,8},{10,11... | collective-permute-start | bytes 1572872 | tf_op jit(solution)/shard_map/ppermute | solution.py:266
  53.9 10.7 %collective-permute-start.15 = (f32[4,64,512]{2,1,0:T(8,128)S(1)}, f32[4,64,512]{2,1,0:T(8,128)S(1)}, u32[]{:S(2)}, u32[]{:S(2)}) collective-permute-start(f32[4,64,512]{2,1,0:T(8,128)S(1)} %get-tuple-element.40), channel_id=1, source_target_pairs={{0,0},{1,2},{2,1},{3,3},{4,4},{5,6},{6,5},{7,7},{8,8},{9,10},{10,9... | collective-permute-start | bytes 1572872 | tf_op jit(solution)/shard_map/ppermute | solution.py:267
  56.9 7.7 %collective-permute-start = (f32[8,512]{1,0:T(8,128)S(1)}, f32[8,512]{1,0:T(8,128)S(1)}, u32[]{:S(2)}, u32[]{:S(2)}) collective-permute-start(f32[8,512]{1,0:T(8,128)S(1)} %copy-done.1), channel_id=1, source_target_pairs={{0,0},{1,2},{2,1},{3,3},{4,4},{5,6},{6,5},{7,7},{8,8},{9,10},{10,9... | collective-permute-start | bytes 49160 | tf_op jit(solution)/shard_map/ppermute | solution.py:255
  59.5 5.1 %collective-permute-start.1 = (f32[8,512]{1,0:T(8,128)S(1)}, f32[8,512]{1,0:T(8,128)S(1)}, u32[]{:S(2)}, u32[]{:S(2)}) collective-permute-start(f32[8,512]{1,0:T(8,128)S(1)} %copy-done.1), channel_id=1, source_target_pairs={{0,1},{1,0},{2,3},{3,2},{4,5},{5,4},{6,7},{7,6},{8,9},{9,8},{10,11... | collective-permute-start | bytes 49160 | tf_op jit(solution)/shard_map/ppermute | solution.py:254

commit v2 on v0

v2 whole, which is shorter than its diff:
```python
import functools

import jax
import jax.numpy as jnp
from jax import lax
from jax.sharding import PartitionSpec as P
from jax.experimental import pallas as pl
from jax.experimental.pallas import tpu as pltpu

TILE = 4
PASSES = 4
diffusion_rate = 0.24
step_scale = 0.5
epsilon = 1e-06
FRAME_BLOCK = 128
LANES = 128
GROUP = 8
TERMS = 3
HIGHEST = lax.Precision.HIGHEST
VMEM = pltpu.VMEM
WHOLE = pl.BlockSpec(memory_space=pltpu.VMEM)
SCALARS = pl.BlockSpec(memory_space=pltpu.SMEM)

CHUNKS = (48, 32)


def barrier(*arrays):
    return lax.optimization_barrier(arrays)


def ranges(slots):
    starts = [sum(slots[:chunk]) for chunk in range(len(slots))]
    return [(start, count // 2) for start, count in zip(starts, slots)]


def iota(shape, dim):
    return lax.broadcasted_iota(jnp.int32, shape, dim)


def active(support, tile, axis):
    return jnp.max(jnp.where(support == tile, 1.0, 0.0), axis=axis, keepdims=True)


def project_kernel(first, chunks, where_ref, support_ref, traces_ref, movie_ref, *refs):
    outs, (held_ref, wide_ref, total_ref, gram_ref, arrived) = refs[:-5], refs[-5:]
    comps, frames = traces_ref.shape
    slots = sum(chunks)
    blocks = arrived.shape[0]
    depth = movie_ref.shape[0] // blocks
    rows = movie_ref.shape[0] // frames
    tiles = rows // TILE
    width = depth // rows

    def copy(block):
        part = pl.ds(block * depth, depth)
        return pltpu.make_async_copy(movie_ref.at[part, :], held_ref.at[part, :], arrived.at[block])

    for block in range(blocks):
        copy(block).start()
    spread = jnp.where(iota((width, depth), 0) == iota((width, depth), 1) // rows, 1.0, 0.0).astype(jnp.bfloat16)
    support = support_ref[...]
    upper = jnp.where(iota((comps, comps), 0) < iota((comps, comps), 1), 1.0, 0.0)
    slot = (iota((slots, comps), 0) + first).astype(jnp.float32)
    select = jnp.zeros((slots, comps), jnp.float32)
    before = jnp.zeros((1, 1), jnp.float32)
    base = jnp.full((slots, 1), -rows, jnp.int32)
    for order in range(tiles):
        tile = jnp.where(lax.rem(where_ref[0], 2) == 0, order, tiles - 1 - order)
        act = active(support, where_ref[0] * tiles + tile, 0)
        rank = jnp.dot(jnp.broadcast_to(act, (8, comps)), upper, preferred_element_type=jnp.float32)[0:1] + before
        select = select + jnp.where(slot == rank, act, 0.0)
        after = before + jnp.sum(act, axis=1, keepdims=True)
        here = (slot[:, 0:1] >= before) & (slot[:, 0:1] < after)
        base = jnp.where(here, TILE * tile, base)
        before = after
    select = select.astype(jnp.bfloat16)
    phase = iota((slots, depth), 1) % rows - base
    traces = traces_ref[...]
    chosen = jnp.dot(select, traces, preferred_element_type=jnp.float32).astype(jnp.bfloat16)
    for block in range(blocks):
        repeated = jnp.dot(
            chosen[:, block * width : (block + 1) * width], spread, preferred_element_type=jnp.float32
        )
        for row in range(TILE):
            wide_ref[row * slots : (row + 1) * slots, block * depth : (block + 1) * depth] = jnp.where(
                phase == row, repeated, 0.0
            ).astype(jnp.bfloat16)
    if first == 0:
        gram_ref[...] = lax.dot_general(
            traces, traces, (((1,), (1,)), ((), ())), preferred_element_type=jnp.float32
        )
    for block in range(blocks):
        copy(block).wait()
        part = jnp.dot(
            wide_ref[:, block * depth : (block + 1) * depth],
            held_ref[block * depth : (block + 1) * depth, :],
            preferred_element_type=jnp.float32,
        )
        if block == 0:
            total_ref[...] = part
        else:
            total_ref[...] += part
    odd = where_ref[1]
    for which in range(2):
        mine = odd if which == 0 else 1 - odd
        for chunk, (begin, half) in enumerate(ranges(chunks)):
            ref = outs[2 * chunk + which]
            for row in range(TILE):
                start = pl.multiple_of(row * slots + begin + mine * half, 8)
                ref[row * half : (row + 1) * half, :] = total_ref[pl.ds(start, half), :]
        if first == 0:
            ref = outs[which]
            filled = TILE * chunks[0] // 2
            band = ref.shape[0] - filled
            ref[filled:, :] = jnp.zeros((band, ref.shape[1]), jnp.float32)
            for piece in range(ref.shape[1] // LANES):
                start = pl.multiple_of((2 * piece + mine) * band, 8)
                ref[filled:, piece * LANES : piece * LANES + comps] = gram_ref[pl.ds(start, band), :]


def project(where, support, traces, recording, first, chunks):
    frames, rows, cols = recording.shape
    comps = traces.shape[0]
    slots = sum(chunks)
    shapes = []
    for chunk, (_, half) in enumerate(ranges(chunks)):
        band = comps * LANES // cols // 2 if first == 0 and chunk == 0 else 0
        shapes += [(TILE * half + band, cols)] * 2
    return pl.pallas_call(
        functools.partial(project_kernel, first, chunks),
        name="project",
        in_specs=[SCALARS, WHOLE, WHOLE, pl.BlockSpec(memory_space=pltpu.HBM)],
        out_specs=[WHOLE] * len(shapes),
        out_shape=[jax.ShapeDtypeStruct(shape, jnp.float32) for shape in shapes],
        scratch_shapes=[
            VMEM((frames * rows, cols), jnp.bfloat16),
            VMEM((TILE * slots, frames * rows), jnp.bfloat16),
            VMEM((TILE * slots, cols), jnp.float32),
            VMEM((comps, comps), jnp.float32),
            pltpu.SemaphoreType.DMA((frames // FRAME_BLOCK,)),
        ],
        compiler_params=pltpu.CompilerParams(vmem_limit_bytes=16 << 20),
    )(where, support, traces, recording.reshape(frames * rows, cols))


def tiles_of(array):
    comps, rows, cols = array.shape
    pieces = array.reshape(comps, rows, cols // LANES, LANES).transpose(0, 2, 1, 3)
    return pieces.reshape(comps * rows * cols // LANES, LANES)


def from_tiles(tiles, comps, rows, cols):
    pieces = tiles.reshape(comps, cols // LANES, rows, LANES).transpose(0, 2, 1, 3)
    return pieces.reshape(comps, rows, cols)


def plane_of(tiles_ref, row, comps, rows, cols):
    step = rows * cols // LANES
    pieces = [tiles_ref[pl.ds(piece * rows + row, comps, stride=step), :] for piece in range(cols // LANES)]
    return jnp.concatenate(pieces, axis=1)


def terms_of(packed):
    terms = []
    for _ in range(TERMS):
        term = packed.astype(jnp.bfloat16)
        packed = packed - term.astype(jnp.float32)
        terms.append(term)
    return jnp.concatenate(terms, axis=0)


def slots_of(ref, half, row):
    height = ref.shape[0] // 2
    return [ref[part * height + row * half : part * height + (row + 1) * half, :] for part in range(2)]


def moved(pick, parts):
    terms = terms_of(jnp.concatenate(parts, axis=0))
    return jnp.dot(pick[:, 0 : terms.shape[0]], terms, preferred_element_type=jnp.float32)


def prepare_kernel(
    count,
    where_ref,
    support_ref,
    sums_ref,
    tiles_ref,
    correlation_ref,
    base_ref,
    pick_ref,
    spare_ref,
    rate_ref,
    outer_ref,
    more_ref,
):
    rows, comps, cols = base_ref.shape
    tiles = rows // TILE
    index = where_ref[0]
    odd = lax.rem(index, 2)
    main = sum(CHUNKS)
    band = comps * LANES // cols // 2
    height = sums_ref.shape[0] // 2
    gram = jnp.concatenate(
        [
            sums_ref[(half + 1) * height - band : (half + 1) * height, piece * LANES : piece * LANES + comps]
            for piece in range(cols // LANES)
            for half in range(2)
        ],
        axis=0,
    )
    own = iota(gram.shape, 0) == iota(gram.shape, 1)
    diagonal = jnp.sum(jnp.where(own, gram, 0.0), axis=1, keepdims=True)
    rate = step_scale / (diagonal + epsilon)
    rate_ref[...] = jnp.broadcast_to(rate, rate_ref.shape)
    support = support_ref[...]
    lower = jnp.where(iota((comps, comps), 1) < iota((comps, comps), 0), 1.0, 0.0)
    place = iota((comps, pick_ref.shape[1]), 1)
    spare = comps * tiles - main

    def terms(count, first):
        return jnp.where(place < TERMS * count, first + place % count, -1).astype(jnp.float32)

    before = jnp.zeros((1, 1), jnp.float32)
    for order in range(tiles):
        tile = jnp.where(odd == 0, order, tiles - 1 - order)
        act = active(support, index * tiles + tile, 1)
        rank = before + jnp.dot(
            lower, jnp.broadcast_to(act, (comps, LANES)), preferred_element_type=jnp.float32
        )[:, 0:1]
        chosen = pl.ds(pl.multiple_of(tile * comps, comps), comps)
        pick_ref[chosen, :] = jnp.where(terms(main, 0) == rank, act, 0.0).astype(jnp.bfloat16)
        spare_ref[chosen, :] = jnp.where(terms(spare, main) == rank, act, 0.0).astype(jnp.bfloat16)
        if order == 0:
            first_pick = jnp.where(terms(CHUNKS[0], 0) == rank, act, 0.0).astype(jnp.bfloat16)
        before = before + jnp.sum(act, axis=0, keepdims=True)
    for row in range(rows):
        act = active(support, index * tiles + row // TILE, 1)
        field = plane_of(tiles_ref, row, comps, rows, cols)
        slope = jnp.dot(gram, field, precision=HIGHEST, preferred_element_type=jnp.float32)
        base_ref[row] = jnp.where(act > 0.0, field - rate * slope, 0.0)
    for row in range(TILE):
        base = jnp.where(odd == 0, base_ref[row], base_ref[rows - TILE + row])
        sums = moved(first_pick, slots_of(sums_ref, CHUNKS[0] // 2, row))
        outer_ref[row * comps : (row + 1) * comps, :] = jnp.maximum(base + rate * sums, 0.0)
    outer_ref[TILE * comps :, :] = correlation_ref[...]
    over = jnp.full((1, 1), -1.0, jnp.float32)
    for device in range(count):
        held = jnp.zeros((1, 1), jnp.float32)
        for tile in range(tiles):
            in_tile = jnp.sum(active(support, device * tiles + tile, 1), axis=0, keepdims=True)
            over = jnp.maximum(over, in_tile - CHUNKS[0])
            held = held + in_tile
        over = jnp.maximum(over, held - main)
    more_ref[0] = (jnp.max(over) > 0.5).astype(jnp.int32)


def prepare(where, support, sums, tiles_in, correlation, count):
    rows = correlation.shape[0]
    comps, cols = support.shape[0], sums.shape[1]
    tiles = rows // TILE
    picks = jax.ShapeDtypeStruct((tiles * comps, 4 * comps), jnp.bfloat16)
    return pl.pallas_call(
        functools.partial(prepare_kernel, count),
        name="prepare",
        in_specs=[SCALARS] + [WHOLE] * 4,
        out_specs=[WHOLE] * 5 + [SCALARS],
        out_shape=[
            jax.ShapeDtypeStruct((rows, comps, cols), jnp.float32),
            picks,
            picks,
            jax.ShapeDtypeStruct((comps, LANES), jnp.float32),
            jax.ShapeDtypeStruct((TILE * comps + rows, cols), jnp.float32),
            jax.ShapeDtypeStruct((1,), jnp.int32),
        ],
        compiler_params=pltpu.CompilerParams(vmem_limit_bytes=12 << 20),
    )(where, support, sums, tiles_in, correlation)


def step_kernel(with_spare, where_ref, base_ref, pick_ref, spare_ref, rate_ref, correlation_ref, *refs):
    refs, outs = refs[: len(CHUNKS) + with_spare], refs[len(CHUNKS) + with_spare :]
    rows, comps, cols = base_ref.shape
    tiles = rows // TILE
    rate = rate_ref[:, 0:1]
    even = lax.rem(where_ref[0], 2) == 0
    for row in range(TILE):
        parts = []
        for ref, (_, half) in zip(refs, ranges(CHUNKS)):
            parts += slots_of(ref, half, row)
        sums = moved(pick_ref, parts)
        if with_spare:
            sums = sums + moved(spare_ref, slots_of(refs[-1], refs[-1].shape[0] // 2 // TILE, row))
        planes = []
        for tile in range(tiles):
            at = tile * TILE + row
            planes.append(jnp.maximum(base_ref[at] + rate * sums[tile * comps : (tile + 1) * comps, :], 0.0))
            outs[0][at] = planes[-1]
        chosen = slice(row * comps, (row + 1) * comps)
        outs[1][chosen, :] = jnp.where(even, planes[-1], planes[0])
        if with_spare:
            outs[2][chosen, :] = jnp.where(even, planes[0], planes[-1])
    for ref in outs[1:]:
        ref[TILE * comps :, :] = correlation_ref[...]


def step_rows(where, prepared, correlation, sums):
    base = prepared[0]
    rows, comps, cols = base.shape
    spare = len(sums) - len(CHUNKS)
    edge = jax.ShapeDtypeStruct((TILE * comps + rows, cols), jnp.float32)
    return pl.pallas_call(
        functools.partial(step_kernel, spare),
        name="step_rows",
        in_specs=[SCALARS] + [WHOLE] * (5 + len(sums)),
        out_specs=[WHOLE] * (2 + spare),
        out_shape=[jax.ShapeDtypeStruct(base.shape, jnp.float32), edge] + [edge] * spare,
        compiler_params=pltpu.CompilerParams(vmem_limit_bytes=12 << 20),
    )(where, *prepared, correlation, *sums)


def diffuse_kernel(
    where_ref,
    support_ref,
    correlation_ref,
    field_ref,
    inner_ref,
    outer_ref,
    out_ref,
    done_ref,
    edge_ref,
    weight_ref,
    keep_ref,
    mask_ref,
    sent,
):
    rows, comps, cols = field_ref.shape
    tiles = rows // TILE
    pieces = cols // LANES
    group = GROUP
    index, last = where_ref[0], where_ref[2]
    odd = lax.rem(index, 2) == 1
    has_above = jnp.where(index > 0, 1.0, 0.0)
    has_below = jnp.where(index < last, 1.0, 0.0)
    for row in range(PASSES):
        chosen = slice(row * comps, (row + 1) * comps)
        inner, outer = inner_ref[chosen, :], outer_ref[chosen, :]
        edge_ref[row] = has_above * jnp.where(odd, inner, outer)
        edge_ref[PASSES + row] = has_below * jnp.where(odd, outer, inner)
    inner, outer = inner_ref[PASSES * comps :, :], outer_ref[PASSES * comps :, :]
    parts = (
        (0, (diffusion_rate * has_above) * jnp.where(odd, inner, outer)[rows - PASSES :]),
        (PASSES, diffusion_rate * correlation_ref[...]),
        (PASSES + rows, (diffusion_rate * has_below) * jnp.where(odd, outer, inner)[:PASSES]),
    )
    for first, weight in parts:
        for row in range(weight.shape[0]):
            line = jnp.broadcast_to(weight[row : row + 1, :], (GROUP, cols))
            weight_ref[first + row] = line
            keep_ref[first + row] = 1.0 - 4.0 * line
    support = support_ref[...]
    for tile in range(tiles):
        act = active(support, index * tiles + tile, 1)
        mask_ref[tile] = jnp.broadcast_to(act, mask_ref.shape[1:])
    lane = iota((group, LANES), 1)
    at_left, at_right = lane == 0, lane == LANES - 1
    nothing = jnp.zeros((group, LANES), jnp.float32)
    total = rows + 2 * PASSES
    size = group * rows * pieces

    def copy(step):
        part = pl.ds(step * size, size)
        return pltpu.make_async_copy(done_ref.at[part, :], out_ref.at[part, :], sent.at[step])

    def relax(step, carry):
        start = pl.multiple_of(step * group, group)
        planes = [{} for _ in range(PASSES + 1)]

        def load(row):
            if row < PASSES:
                ref, at = edge_ref, row
            elif row < PASSES + rows:
                ref, at = field_ref, row - PASSES
            else:
                ref, at = edge_ref, row - rows
            return [ref[at, pl.ds(start, group), piece * LANES : (piece + 1) * LANES] for piece in range(pieces)]

        def renew(done, row):
            above, center, below = (planes[done][row + shift] for shift in (-1, 0, 1))
            to_right = [pltpu.roll(piece, 1, 1) for piece in center]
            to_left = [pltpu.roll(piece, LANES - 1, 1) for piece in center]
            fresh = []
            for piece in range(pieces):
                left = jnp.where(at_left, to_right[piece - 1] if piece > 0 else nothing, to_right[piece])
                right = jnp.where(at_right, to_left[piece + 1] if piece < pieces - 1 else nothing, to_left[piece])
                beside = (above[piece] + below[piece]) + (left + right)
                lanes = slice(piece * LANES, (piece + 1) * LANES)
                fresh.append(keep_ref[row, :, lanes] * center[piece] + weight_ref[row, :, lanes] * beside)
            return fresh

        masks = [mask_ref[tile, pl.ds(start, group), :] for tile in range(tiles)]
        for front in range(total + PASSES):
            if front < total:
                planes[0][front] = load(front)
            for done in range(PASSES):
                row = front - 1 - done
                if done < row < total - 1 - done:
                    planes[done + 1][row] = renew(done, row)
                    planes[done].pop(row - 1)
                    if done == PASSES - 1:
                        own = row - PASSES
                        for piece in range(pieces):
                            at = pl.ds(step * size + piece * rows + own, group, stride=rows * pieces)
                            done_ref[at, :] = planes[PASSES][row][piece] * masks[own // TILE]
        copy(step).start()
        return carry

    lax.fori_loop(0, comps // group, relax, 0)
    for step in range(comps // group):
        copy(step).wait()


def diffuse(where, support, correlation, field, inner, outer):
    rows, comps, cols = field.shape
    pieces = cols // LANES
    lines = VMEM((rows + 2 * PASSES, GROUP, cols), jnp.float32)
    shape = (comps * rows * pieces, LANES)
    return pl.pallas_call(
        diffuse_kernel,
        name="diffuse",
        in_specs=[SCALARS] + [WHOLE] * 5,
        out_specs=pl.BlockSpec(memory_space=pltpu.HBM),
        out_shape=jax.ShapeDtypeStruct(shape, jnp.float32),
        scratch_shapes=[
            VMEM(shape, jnp.float32),
            VMEM((2 * PASSES, comps, cols), jnp.float32),
            lines,
            lines,
            VMEM((rows // TILE, comps, LANES), jnp.float32),
            pltpu.SemaphoreType.DMA((comps // GROUP,)),
        ],
        compiler_params=pltpu.CompilerParams(vmem_limit_bytes=16 << 20),
    )(where, support, correlation, field, inner, outer)


def pairs_of(count, first):
    table = list(range(count))
    for i in range(first, count - 1, 2):
        table[i], table[i + 1] = i + 1, i
    return list(enumerate(table))


NEAR, FAR = pairs_of(4, 0), [(0, 3), (1, 2), (2, 1), (3, 0)]


def in_order(odd, mine, other):
    return jnp.concatenate([jnp.where(odd, other, mine), jnp.where(odd, mine, other)], axis=0)


def per_device(recording, traces, footprints, correlation, support):
    comps, rows, cols = footprints.shape
    tiles = rows // TILE
    index = lax.axis_index("rows")
    count = lax.axis_size("rows")
    part = lax.axis_index("tm")
    line = lax.axis_size("tm") == 4
    odd = ((part == 1) | (part == 2)) & line
    where = jnp.stack([index, odd.astype(jnp.int32), jnp.int32(count - 1)]).astype(jnp.int32)
    inside, outside = pairs_of(count, 0), pairs_of(count, 1)
    names = support.T
    field_tiles = tiles_of(footprints)
    spare = comps * tiles - sum(CHUNKS)

    def near(array):
        return lax.ppermute(array, "tm", NEAR)

    def far(array):
        return lax.ppermute(array, "tm", FAR)

    def beside(array):
        return lax.ppermute(array, "rows", outside)

    mine, other = [None, None], [None, None]
    mine[0], other[0] = project(where, names, traces, recording, 0, CHUNKS[:1])
    *_, later = barrier(other[0], traces)
    mine[1], other[1] = project(where, names, later, recording, CHUNKS[0], CHUNKS[1:])
    if line:
        first_received = near(other[0])
        half = [barrier(mine[0] + first_received)[0]]
        later, half[0] = barrier(other[1], half[0])
        first_across = far(half[0])
        half.append(barrier(mine[1] + near(later))[0])
        whole = [barrier(half[0] + first_across)[0]]
        half[1], whole[0] = barrier(half[1], whole[0])
        first_back = near(whole[0])
        whole.append(barrier(half[1] + far(half[1]))[0])
        back = [first_back, near(whole[1])]
    else:
        whole, back = lax.psum((mine, other), "tm")
    sums = [barrier(in_order(odd, *barrier(whole[0], back[0])))[0]]
    *prepared, to_outer, more = prepare(where, support, sums[0], field_tiles, correlation, count)
    outer = beside(to_outer)
    own, theirs, *prepared = barrier(whole[1], back[1], *prepared)
    sums.append(barrier(in_order(odd, own, theirs))[0])

    def rest():
        mine, other = project(where, names, traces, recording, sum(CHUNKS), (spare,))
        if line:
            half = mine + near(other)
            mine = half + far(half)
            other = near(mine)
        else:
            mine, other = lax.psum((mine, other), "tm")
        field, to_inner, to_outer = step_rows(where, prepared, correlation, sums + [in_order(odd, mine, other)])
        return field, to_inner, beside(to_outer)

    def enough():
        field, to_inner = step_rows(where, prepared, correlation, sums)
        return field, to_inner, outer

    field, to_inner, outer = lax.cond(more[0] > 0, rest, enough)
    inner = lax.ppermute(to_inner, "rows", inside)
    result = diffuse(where, support, correlation, field, inner, outer)
    return from_tiles(result, comps, rows, cols)


def solution(mesh):
    return jax.shard_map(
        per_device,
        mesh=mesh,
        in_specs=(
            P("tm", ("band", "rows"), None),
            P("band", "tm"),
            P(None, ("band", "rows"), None),
            P(("band", "rows"), None),
            P("band", None),
        ),
        out_specs=P(None, ("band", "rows"), None),
        check_vma=False,
    )
```

time: 113 us -> 56.6 us (0.50)
  waiting for transfers between devices: 45 us -> 24.6 us
  Pallas kernels: 0 us -> 19.6 us
  blocking collectives: 16.9 us -> 0 us
  local copies, waits for them, and re-layouts: 16.7 us -> 0.11 us
  between operations: 13.6 us -> 0.71 us
  matrix products: 8.54 us -> 0 us
  other arithmetic: 6.57 us -> 0.28 us
  starting transfers between devices: 5.55 us -> 11 us
    psum x1 -> x0, waiting for transfers between devices: 36.2 us -> none  [per_device(): gram_matrix, projected = lax.psum((gram_part, product), 'tm')]
    pallas_call x0 -> x5, Pallas kernels: none -> 19.6 us  [the longest x2 9.04 us: project(): pl.pallas_call(functools.partial(project_kernel, first, chunks), name='pr...]
    psum x1 -> x0, blocking collectives: 16.9 us -> none  [per_device(): gram_matrix, projected = lax.psum((gram_part, product), 'tm')]
    ppermute x2 -> x8, waiting for transfers between devices: 8.73 us -> 24.6 us  [the longest x4 20.6 us: near(): return lax.ppermute(array, 'tm', NEAR)]
    unnamed x11, local copies, waits for them, and re-layouts: 13.5 us -> 0.11 us
    dot_general x3 -> x0, matrix products: 8.54 us -> none  [the longest x1 6.01 us: per_device(): product = jnp.dot(traces, flattened, preferred_element_type=jnp.float32)]
    ppermute x2 -> x8, starting transfers between devices: 5.55 us -> 11 us  [the longest x1 4.32 us: beside(): return lax.ppermute(array, 'rows', outside)]
    add x4, other arithmetic: 3.96 us -> 0.1 us  [the longest x1 0.03 us: per_device(): whole = [barrier(half[0] + first_across)[0]]]
  transfers between devices with their start and end apart: 3 -> 8, of which waited for: 3 -> 6; matrix products, arithmetic and copies ran while one was open for 2% -> 0% of each run, Pallas kernels for 0% -> 10%
where the time goes in v2:
time: 56.6 us; the launch traced here: 56.3 us
  waiting for transfers between devices  24.6 us (43%)
  Pallas kernels  19.6 us (35%)
  starting transfers between devices  11 us (19%)
  between operations  0.71 us (1%)
    ppermute x4, waiting for transfers between devices, near(): return lax.ppermute(array, 'tm', NEAR)  20.6 us
    pallas_call x2, Pallas kernels, project(): pl.pallas_call(functools.partial(project_kernel, first, chunks), name='pr...  9.04 us
    pallas_call x1, Pallas kernels, diffuse(): pl.pallas_call(diffuse_kernel, name='diffuse', in_specs=[SCALARS] + [WHOL...  7.39 us
    ppermute x1, starting transfers between devices, beside(): return lax.ppermute(array, 'rows', outside)  4.32 us
    ppermute x2, starting transfers between devices, far(): return lax.ppermute(array, 'tm', FAR)  3.42 us
    ppermute x4, starting transfers between devices, near(): return lax.ppermute(array, 'tm', NEAR)  3.14 us
    pallas_call x1, Pallas kernels, prepare(): pl.pallas_call(functools.partial(prepare_kernel, count), name='prepare',...  2.36 us
    ppermute x1, waiting for transfers between devices, beside(): return lax.ppermute(array, 'rows', outside)  2.04 us
  transfers between devices with their start and end apart: 8, of which 6 were waited for; matrix products, arithmetic and copies ran while one was open for 0% of the time, Pallas kernels for 10%

profile of v2, /device:TPU:1, one launch (start us, length us, event | category | flops | bytes accessed | tf_op | source)
XLA Modules:
  0.0 56.3 jit_solution(5577198495690555116)
XLA Ops:
  0.0 0.0 copy-start.2
  0.0 0.0 copy-start.4
  0.0 0.0 copy-start.1
  0.0 0.1 pad_add_fusion.where_ref
  0.1 0.0 copy-start
  0.1 0.0 copy-start.3
  0.1 5.5 %project.4 = (f32[104,512]{1,0:T(8,128)S(1)}, f32[104,512]{1,0:T(8,128)S(1)}) custom-call(s32[3]{0:T(128)S(1)} %pad_add_fusion.where_ref, s32[4,64]{1,0:T(4,128)} %bitcast.20, bf16[64,1024]{1,0:T(8,128)(2,1)} %traces_ref.2, bf16[8192,512]{1,0:T(8,128)(2,1)} %bitcast.17), custom_call_target="tpu_custom_call" | custom-call | tf_op jit(solution)/shard_map/project/pallas_call | solution.py:129
  5.6 2.2 %collective-permute-start.4 = (f32[104,512]{1,0:T(8,128)S(1)}, f32[104,512]{1,0:T(8,128)S(1)}, u32[]{:S(2)}, u32[]{:S(2)}) collective-permute-start(f32[104,512]{1,0:T(8,128)S(1)} %get-tuple-element.101), channel_id=1, source_target_pairs={{0,4},{4,0},{8,12},{12,8},{1,5},{5,1},{9,13},{13,9},{2,6},{6,2},{1... | collective-permute-start | bytes 638984 | tf_op jit(solution)/shard_map/ppermute | solution.py:473
  7.8 0.0 copy-done.2
  7.8 0.0 copy-done.4
  7.8 0.0 copy-done.1
  7.8 3.5 %project.5 = (f32[64,512]{1,0:T(8,128)S(1)}, f32[64,512]{1,0:T(8,128)S(1)}) custom-call(s32[3]{0:T(128)S(1)} %pad_add_fusion.where_ref, s32[4,64]{1,0:T(4,128)S(1)} %bitcast.21, bf16[64,1024]{1,0:T(8,128)(2,1)S(1)} %copy-done.2, bf16[8192,512]{1,0:T(8,128)(2,1)S(1)} %bitcast.18), custom_call_target="tpu_custom_call" | custom-call | tf_op jit(solution)/shard_map/project/pallas_call | solution.py:129
  11.3 1.5 %collective-permute-done.4 = f32[104,512]{1,0:T(8,128)S(1)} collective-permute-done((f32[104,512]{1,0:T(8,128)S(1)}, f32[104,512]{1,0:T(8,128)S(1)}, u32[]{:S(2)}, u32[]{:S(2)}) %collective-permute-start.4) | collective-permute-done | bytes 213024 | tf_op jit(solution)/shard_map/ppermute | solution.py:473
  12.8 3.2 %collective-permute-start.6 = (f32[104,512]{1,0:T(8,128)S(1)}, f32[104,512]{1,0:T(8,128)S(1)}, u32[]{:S(2)}, u32[]{:S(2)}) collective-permute-start(f32[104,512]{1,0:T(8,128)S(1)} %add.18), channel_id=1, source_target_pairs={{0,12},{4,8},{8,4},{12,0},{1,13},{5,9},{9,5},{13,1},{2,14},{6,10},... | collective-permute-start | bytes 638984 | tf_op jit(solution)/shard_map/ppermute | solution.py:476
  16.1 0.0 collective-permute-start.5
  16.1 8.5 %collective-permute-done.5 = f32[64,512]{1,0:T(8,128)S(1)} collective-permute-done((f32[64,512]{1,0:T(8,128)S(1)}, f32[64,512]{1,0:T(8,128)S(1)}, u32[]{:S(2)}, u32[]{:S(2)}) %collective-permute-start.5) | collective-permute-done | bytes 131104 | tf_op jit(solution)/shard_map/ppermute | solution.py:473
  24.6 0.0 collective-permute-done.6
  24.6 0.3 collective-permute-start.7
  24.9 0.1 copy.7.support_ref
  25.0 0.2 collective-permute-start.8
  25.1 7.0 %collective-permute-done.7 = f32[104,512]{1,0:T(8,128)S(1)} collective-permute-done((f32[104,512]{1,0:T(8,128)S(1)}, f32[104,512]{1,0:T(8,128)S(1)}, u32[]{:S(2)}, u32[]{:S(2)}) %collective-permute-start.7) | collective-permute-done | bytes 213024 | tf_op jit(solution)/shard_map/ppermute | solution.py:473
  32.2 0.0 copy-done
  32.2 0.0 copy-done.3
  32.2 2.4 %prepare.1 = (f32[8,64,512]{2,1,0:T(8,128)S(1)}, bf16[128,256]{1,0:T(8,128)(2,1)S(1)}, bf16[128,256]{1,0:T(8,128)(2,1)S(1)}, f32[64,128]{1,0:T(8,128)S(1)}, f32[264,512]{1,0:T(8,128)S(1)}, /*index=5*/s32[1]{0:T(128)}) custom-call(s32[3]{0:T(128)S(1)} %pad_add_fusion.where_ref, s32[64,4]{1,0:T(8,128)S(1)} %copy.7.support_ref, ...), custom_call_target="tpu_custom_call" | custom-call | tf_op jit(solution)/shard_map/prepare/pallas_call | solution.py:262
  34.6 4.3 %collective-permute-start.10 = (f32[264,512]{1,0:T(8,128)S(1)}, f32[264,512]{1,0:T(8,128)}, u32[]{:S(2)}, u32[]{:S(2)}) collective-permute-start(f32[264,512]{1,0:T(8,128)S(1)} %get-tuple-element.123), channel_id=1, source_target_pairs={{0,0},{1,2},{2,1},{3,3},{4,4},{5,6},{6,5},{7,7},{8,8},{9,10},{10,9... | collective-permute-start | bytes 1622024 | tf_op jit(solution)/shard_map/ppermute | solution.py:479
  38.9 0.0 collective-permute-done.8
  38.9 0.7 %collective-permute-start.9 = (f32[64,512]{1,0:T(8,128)S(1)}, f32[64,512]{1,0:T(8,128)S(1)}, u32[]{:S(2)}, u32[]{:S(2)}) collective-permute-start(f32[64,512]{1,0:T(8,128)S(1)} %add.21), channel_id=1, source_target_pairs={{0,4},{4,0},{8,12},{12,8},{1,5},{5,1},{9,13},{13,9},{2,6},{6,2},{1... | collective-permute-start | bytes 393224 | tf_op jit(solution)/shard_map/ppermute | solution.py:473
  40.2 3.7 %collective-permute-done.9 = f32[64,512]{1,0:T(8,128)S(1)} collective-permute-done((f32[64,512]{1,0:T(8,128)S(1)}, f32[64,512]{1,0:T(8,128)S(1)}, u32[]{:S(2)}, u32[]{:S(2)}) %collective-permute-start.9) | collective-permute-done | bytes 131104 | tf_op jit(solution)/shard_map/ppermute | solution.py:473
  44.0 2.0 %collective-permute-done.10 = f32[264,512]{1,0:T(8,128)} collective-permute-done((f32[264,512]{1,0:T(8,128)S(1)}, f32[264,512]{1,0:T(8,128)}, u32[]{:S(2)}, u32[]{:S(2)}) %collective-permute-start.10) | collective-permute-done | bytes 540704 | tf_op jit(solution)/shard_map/ppermute | solution.py:479
  46.0 0.9 %conditional.1 = (f32[8,64,512]{2,1,0:T(8,128)S(1)}, f32[264,512]{1,0:T(8,128)S(1)}, f32[264,512]{1,0:T(8,128)}) conditional(s32[]{:T(128)} %bitcast.8, (s32[3]{0:T(128)S(1)}, f32[8,64,512]{2,1,0:T(8,128)S(1)}, bf16[128,256]{1,0:T(8,128)(2,1)S(1)}, bf16[128,256]{1,0:T(8,128)(2,1)S(1)}, f32[64,128]{1,0:T(8,128)S(1)}, ...), branch_computations={%region_0.1_spmd, %region_1.2_spmd} | conditional | flops 294912 | bytes 7274681 | solution.py:519
  46.0 0.9 %step_rows.2 = (f32[8,64,512]{2,1,0:T(8,128)S(1)}, f32[264,512]{1,0:T(8,128)S(1)}) custom-call(s32[3]{0:T(128)S(1)} %get-tuple-element.47.where_ref, f32[8,64,512]{2,1,0:T(8,128)S(1)} %get-tuple-element.48.base_ref, bf16[128,256]{1,0:T(8,128)(2,1)S(1)} %get-tuple-element.49.pick_ref, bf16[128,256]{1,0:T(8,128)(2,1)S(1)} %get-tuple-element.50.spare_ref, ...), custom_call_target="tpu_custom_call" | custom-call | tf_op jit(solution)/shard_map/cond/branch_0_fun/step_rows/pallas_call | solution.py:310
  46.9 0.1 collective-permute-start.11
  47.0 1.9 %collective-permute-done.11.inner_ref = f32[264,512]{1,0:T(8,128)S(1)} collective-permute-done((f32[264,512]{1,0:T(8,128)S(1)}, f32[264,512]{1,0:T(8,128)S(1)}, u32[]{:S(2)}, u32[]{:S(2)}) %collective-permute-start.11) | collective-permute-done | bytes 540704 | tf_op jit(solution)/shard_map/ppermute | solution.py:520
  48.9 7.4 %diffuse.1 = f32[2048,128]{1,0:T(8,128)} custom-call(s32[3]{0:T(128)S(1)} %pad_add_fusion.where_ref, s32[64,4]{1,0:T(8,128)S(1)} %copy.7.support_ref, f32[8,512]{1,0:T(8,128)S(1)} %copy-done.3, f32[8,64,512]{2,1,0:T(8,128)S(1)} %get-tuple-element.124.field_ref, f32[264,512]{1,0:T(8,128)S(1)} %collective-permute-done.11.inner_ref, ...), custom_call_target="tpu_custom_call" | custom-call | tf_op jit(solution)/shard_map/diffuse/pallas_call | solution.py:426
  (8 shorter events, 0.2 us)
Async XLA Ops:
  0.0 7.8 %copy-start.2 = (bf16[64,1024]{1,0:T(8,128)(2,1)S(1)}, bf16[64,1024]{1,0:T(8,128)(2,1)}, u32[]{:S(2)}) copy-start(bf16[64,1024]{1,0:T(8,128)(2,1)} %traces_ref.2) | copy-start | bytes 393220
  0.0 7.8 %copy-start.4 = (s32[64,4]{0,1:T(4,128)S(1)}, s32[64,4]{0,1:T(4,128)}, u32[]{:S(2)}) copy-start(s32[64,4]{0,1:T(4,128)} %param.11) | copy-start | bytes 3076
  0.0 7.8 %copy-start.1 = (bf16[1024,8,512]{2,1,0:T(8,128)(2,1)S(1)}, bf16[1024,8,512]{2,1,0:T(8,128)(2,1)}, u32[]{:S(2)}) copy-start(bf16[1024,8,512]{2,1,0:T(8,128)(2,1)} %param.7) | copy-start | bytes 25165828
  0.1 32.1 %copy-start = (f32[64,8,512]{2,1,0:T(8,128)S(1)}, f32[64,8,512]{2,1,0:T(8,128)}, u32[]{:S(2)}) copy-start(f32[64,8,512]{2,1,0:T(8,128)} %param.9) | copy-start | bytes 3145732
  0.1 32.1 %copy-start.3 = (f32[8,512]{1,0:T(8,128)S(1)}, f32[8,512]{1,0:T(8,128)}, u32[]{:S(2)}) copy-start(f32[8,512]{1,0:T(8,128)} %correlation_ref.3) | copy-start | bytes 49156
  5.6 7.1 %collective-permute-start.4 = (f32[104,512]{1,0:T(8,128)S(1)}, f32[104,512]{1,0:T(8,128)S(1)}, u32[]{:S(2)}, u32[]{:S(2)}) collective-permute-start(f32[104,512]{1,0:T(8,128)S(1)} %get-tuple-element.101), channel_id=1, source_target_pairs={{0,4},{4,0},{8,12},{12,8},{1,5},{5,1},{9,13},{13,9},{2,6},{6,2},{1... | collective-permute-start | bytes 638984 | tf_op jit(solution)/shard_map/ppermute | solution.py:473
  12.8 11.7 %collective-permute-start.6 = (f32[104,512]{1,0:T(8,128)S(1)}, f32[104,512]{1,0:T(8,128)S(1)}, u32[]{:S(2)}, u32[]{:S(2)}) collective-permute-start(f32[104,512]{1,0:T(8,128)S(1)} %add.18), channel_id=1, source_target_pairs={{0,12},{4,8},{8,4},{12,0},{1,13},{5,9},{9,5},{13,1},{2,14},{6,10},... | collective-permute-start | bytes 638984 | tf_op jit(solution)/shard_map/ppermute | solution.py:476
  16.1 8.5 %collective-permute-start.5 = (f32[64,512]{1,0:T(8,128)S(1)}, f32[64,512]{1,0:T(8,128)S(1)}, u32[]{:S(2)}, u32[]{:S(2)}) collective-permute-start(f32[64,512]{1,0:T(8,128)S(1)} %get-tuple-element.106), channel_id=1, source_target_pairs={{0,4},{4,0},{8,12},{12,8},{1,5},{5,1},{9,13},{13,9},{2,6},{6,2},{1... | collective-permute-start | bytes 393224 | tf_op jit(solution)/shard_map/ppermute | solution.py:473
  24.6 7.5 %collective-permute-start.7 = (f32[104,512]{1,0:T(8,128)S(1)}, f32[104,512]{1,0:T(8,128)S(1)}, u32[]{:S(2)}, u32[]{:S(2)}) collective-permute-start(f32[104,512]{1,0:T(8,128)S(1)} %add.20), channel_id=1, source_target_pairs={{0,4},{4,0},{8,12},{12,8},{1,5},{5,1},{9,13},{13,9},{2,6},{6,2},{1... | collective-permute-start | bytes 638984 | tf_op jit(solution)/shard_map/ppermute | solution.py:473
  25.0 14.0 %collective-permute-start.8 = (f32[64,512]{1,0:T(8,128)S(1)}, f32[64,512]{1,0:T(8,128)S(1)}, u32[]{:S(2)}, u32[]{:S(2)}) collective-permute-start(f32[64,512]{1,0:T(8,128)S(1)} %add.19), channel_id=1, source_target_pairs={{0,12},{4,8},{8,4},{12,0},{1,13},{5,9},{9,5},{13,1},{2,14},{6,10},... | collective-permute-start | bytes 393224 | tf_op jit(solution)/shard_map/ppermute | solution.py:476
  34.6 11.5 %collective-permute-start.10 = (f32[264,512]{1,0:T(8,128)S(1)}, f32[264,512]{1,0:T(8,128)}, u32[]{:S(2)}, u32[]{:S(2)}) collective-permute-start(f32[264,512]{1,0:T(8,128)S(1)} %get-tuple-element.123), channel_id=1, source_target_pairs={{0,0},{1,2},{2,1},{3,3},{4,4},{5,6},{6,5},{7,7},{8,8},{9,10},{10,9... | collective-permute-start | bytes 1622024 | tf_op jit(solution)/shard_map/ppermute | solution.py:479
  38.9 5.0 %collective-permute-start.9 = (f32[64,512]{1,0:T(8,128)S(1)}, f32[64,512]{1,0:T(8,128)S(1)}, u32[]{:S(2)}, u32[]{:S(2)}) collective-permute-start(f32[64,512]{1,0:T(8,128)S(1)} %add.21), channel_id=1, source_target_pairs={{0,4},{4,0},{8,12},{12,8},{1,5},{5,1},{9,13},{13,9},{2,6},{6,2},{1... | collective-permute-start | bytes 393224 | tf_op jit(solution)/shard_map/ppermute | solution.py:473
  46.9 2.0 %collective-permute-start.11 = (f32[264,512]{1,0:T(8,128)S(1)}, f32[264,512]{1,0:T(8,128)S(1)}, u32[]{:S(2)}, u32[]{:S(2)}) collective-permute-start(f32[264,512]{1,0:T(8,128)S(1)} %get-tuple-element.125), channel_id=1, source_target_pairs={{0,1},{1,0},{2,3},{3,2},{4,5},{5,4},{6,7},{7,6},{8,9},{9,8},{10,11... | collective-permute-start | bytes 1622024 | tf_op jit(solution)/shard_map/ppermute | solution.py:520

commit v3 on v2

--- a/solution.py
+++ b/solution.py
@@ -139,7 +139,7 @@
             VMEM((comps, comps), jnp.float32),
             pltpu.SemaphoreType.DMA((frames // FRAME_BLOCK,)),
         ],
-        compiler_params=pltpu.CompilerParams(vmem_limit_bytes=16 << 20),
+        compiler_params=pltpu.CompilerParams(vmem_limit_bytes=13 << 20),
     )(where, support, traces, recording.reshape(frames * rows, cols))
 
 
@@ -179,25 +179,8 @@
     return jnp.dot(pick[:, 0 : terms.shape[0]], terms, preferred_element_type=jnp.float32)
 
 
-def prepare_kernel(
-    count,
-    where_ref,
-    support_ref,
-    sums_ref,
-    tiles_ref,
-    correlation_ref,
-    base_ref,
-    pick_ref,
-    spare_ref,
-    rate_ref,
-    outer_ref,
-    more_ref,
-):
-    rows, comps, cols = base_ref.shape
-    tiles = rows // TILE
-    index = where_ref[0]
-    odd = lax.rem(index, 2)
-    main = sum(CHUNKS)
+def gram_of(sums_ref, comps):
+    cols = sums_ref.shape[1]
     band = comps * LANES // cols // 2
     height = sums_ref.shape[0] // 2
     gram = jnp.concatenate(
@@ -210,39 +193,49 @@
     )
     own = iota(gram.shape, 0) == iota(gram.shape, 1)
     diagonal = jnp.sum(jnp.where(own, gram, 0.0), axis=1, keepdims=True)
-    rate = step_scale / (diagonal + epsilon)
-    rate_ref[...] = jnp.broadcast_to(rate, rate_ref.shape)
+    return gram, step_scale / (diagonal + epsilon)
+
+
+def descend(gram, rate, field, act):
+    slope = jnp.dot(gram, field, precision=HIGHEST, preferred_element_type=jnp.float32)
+    return jnp.where(act > 0.0, field - rate * slope, 0.0)
+
+
+def rank_of(act):
+    comps = act.shape[0]
+    lower = jnp.where(iota((comps, comps), 1) < iota((comps, comps), 0), 1.0, 0.0)
+    return jnp.dot(lower, jnp.broadcast_to(act, (comps, LANES)), preferred_element_type=jnp.float32)[:, 0:1]
+
+
+def term_slots(comps, count, first):
+    place = iota((comps, 4 * comps), 1)
+    return jnp.where(place < TERMS * count, first + place % count, -1).astype(jnp.float32)
+
+
+def plan_kernel(
+    count, where_ref, support_ref, tiles_ref, planes_ref, act_ref, first_ref, pick_ref, spare_ref, more_ref
+):
+    rows, comps, cols = planes_ref.shape
+    tiles = rows // TILE
+    index = where_ref[0]
+    main = sum(CHUNKS)
+    spare = comps * tiles - main
     support = support_ref[...]
-    lower = jnp.where(iota((comps, comps), 1) < iota((comps, comps), 0), 1.0, 0.0)
-    place = iota((comps, pick_ref.shape[1]), 1)
-    spare = comps * tiles - main
-
-    def terms(count, first):
-        return jnp.where(place < TERMS * count, first + place % count, -1).astype(jnp.float32)
-
+    for row in range(rows):
+        planes_ref[row] = plane_of(tiles_ref, row, comps, rows, cols)
     before = jnp.zeros((1, 1), jnp.float32)
     for order in range(tiles):
-        tile = jnp.where(odd == 0, order, tiles - 1 - order)
+        tile = jnp.where(lax.rem(index, 2) == 0, order, tiles - 1 - order)
         act = active(support, index * tiles + tile, 1)
-        rank = before + jnp.dot(
-            lower, jnp.broadcast_to(act, (comps, LANES)), preferred_element_type=jnp.float32
-        )[:, 0:1]
+        act_ref[tile] = jnp.broadcast_to(act, (comps, LANES))
+        rank = before + rank_of(act)
         chosen = pl.ds(pl.multiple_of(tile * comps, comps), comps)
-        pick_ref[chosen, :] = jnp.where(terms(main, 0) == rank, act, 0.0).astype(jnp.bfloat16)
-        spare_ref[chosen, :] = jnp.where(terms(spare, main) == rank, act, 0.0).astype(jnp.bfloat16)
+        pick_ref[chosen, :] = jnp.where(term_slots(comps, main, 0) == rank, act, 0.0).astype(jnp.bfloat16)
+        spare_ref[chosen, :] = jnp.where(term_slots(comps, spare, main) == rank, act, 0.0).astype(jnp.bfloat16)
         if order == 0:
-            first_pick = jnp.where(terms(CHUNKS[0], 0) == rank, act, 0.0).astype(jnp.bfloat16)
+            first = jnp.where(term_slots(comps, CHUNKS[0], 0) == rank, act, 0.0)
+            first_ref[...] = first.astype(jnp.bfloat16)
         before = before + jnp.sum(act, axis=0, keepdims=True)
-    for row in range(rows):
-        act = active(support, index * tiles + row // TILE, 1)
-        field = plane_of(tiles_ref, row, comps, rows, cols)
-        slope = jnp.dot(gram, field, precision=HIGHEST, preferred_element_type=jnp.float32)
-        base_ref[row] = jnp.where(act > 0.0, field - rate * slope, 0.0)
-    for row in range(TILE):
-        base = jnp.where(odd == 0, base_ref[row], base_ref[rows - TILE + row])
-        sums = moved(first_pick, slots_of(sums_ref, CHUNKS[0] // 2, row))
-        outer_ref[row * comps : (row + 1) * comps, :] = jnp.maximum(base + rate * sums, 0.0)
-    outer_ref[TILE * comps :, :] = correlation_ref[...]
     over = jnp.full((1, 1), -1.0, jnp.float32)
     for device in range(count):
         held = jnp.zeros((1, 1), jnp.float32)
@@ -254,26 +247,76 @@
     more_ref[0] = (jnp.max(over) > 0.5).astype(jnp.int32)
 
 
-def prepare(where, support, sums, tiles_in, correlation, count):
-    rows = correlation.shape[0]
-    comps, cols = support.shape[0], sums.shape[1]
+def plan(where, support, tiles_in, rows, count):
+    comps = support.shape[0]
+    cols = tiles_in.shape[0] * LANES // (rows * comps)
     tiles = rows // TILE
-    picks = jax.ShapeDtypeStruct((tiles * comps, 4 * comps), jnp.bfloat16)
+
+    def picks(number):
+        return jax.ShapeDtypeStruct((number * comps, 4 * comps), jnp.bfloat16)
+
     return pl.pallas_call(
-        functools.partial(prepare_kernel, count),
-        name="prepare",
-        in_specs=[SCALARS] + [WHOLE] * 4,
+        functools.partial(plan_kernel, count),
+        name="plan",
+        in_specs=[SCALARS] + [WHOLE] * 2,
         out_specs=[WHOLE] * 5 + [SCALARS],
         out_shape=[
             jax.ShapeDtypeStruct((rows, comps, cols), jnp.float32),
-            picks,
-            picks,
-            jax.ShapeDtypeStruct((comps, LANES), jnp.float32),
-            jax.ShapeDtypeStruct((TILE * comps + rows, cols), jnp.float32),
+            jax.ShapeDtypeStruct((tiles, comps, LANES), jnp.float32),
+            picks(1),
+            picks(tiles),
+            picks(tiles),
             jax.ShapeDtypeStruct((1,), jnp.int32),
         ],
-        compiler_params=pltpu.CompilerParams(vmem_limit_bytes=12 << 20),
-    )(where, support, sums, tiles_in, correlation)
+        compiler_params=pltpu.CompilerParams(vmem_limit_bytes=6 << 20),
+    )(where, support, tiles_in)
+
+
+def edge_kernel(where_ref, sums_ref, planes_ref, act_ref, first_ref, correlation_ref, outer_ref):
+    rows, comps, cols = planes_ref.shape
+    odd = lax.rem(where_ref[0], 2)
+    gram, rate = gram_of(sums_ref, comps)
+    act = act_ref[odd * (rows // TILE - 1)][:, 0:1]
+    for row in range(TILE):
+        field = planes_ref[odd * (rows - TILE) + row]
+        sums = moved(first_ref, slots_of(sums_ref, CHUNKS[0] // 2, row))
+        field = jnp.maximum(descend(gram, rate, field, act) + rate * sums, 0.0)
+        outer_ref[row * comps : (row + 1) * comps, :] = field
+    outer_ref[TILE * comps :, :] = correlation_ref[...]
+
+
+def edge_rows(where, sums, planes, act, first, correlation):
+    rows, comps, cols = planes.shape
+    return pl.pallas_call(
+        edge_kernel,
+        name="edge_rows",
+        in_specs=[SCALARS] + [WHOLE] * 5,
+        out_specs=WHOLE,
+        out_shape=jax.ShapeDtypeStruct((TILE * comps + rows, cols), jnp.float32),
+        compiler_params=pltpu.CompilerParams(vmem_limit_bytes=6 << 20),
+    )(where, sums, planes, act, first, correlation)
+
+
+def prepare_kernel(sums_ref, planes_ref, act_ref, base_ref, rate_ref):
+    rows, comps, cols = base_ref.shape
+    gram, rate = gram_of(sums_ref, comps)
+    rate_ref[...] = jnp.broadcast_to(rate, rate_ref.shape)
+    for row in range(rows):
+        base_ref[row] = descend(gram, rate, planes_ref[row], act_ref[row // TILE][:, 0:1])
+
+
+def prepare(sums, planes, act):
+    return pl.pallas_call(
+        prepare_kernel,
+        name="prepare",
+        in_specs=[WHOLE] * 3,
+        out_specs=[WHOLE] * 2,
+        out_shape=[
+            jax.ShapeDtypeStruct(planes.shape, jnp.float32),
+            jax.ShapeDtypeStruct((planes.shape[1], LANES), jnp.float32),
+        ],
+        compiler_params=pltpu.CompilerParams(vmem_limit_bytes=6 << 20),
+    )(sums, planes, act)
 
 
 def step_kernel(with_spare, where_ref, base_ref, pick_ref, spare_ref, rate_ref, correlation_ref, *refs):
@@ -296,8 +339,7 @@
             outs[0][at] = planes[-1]
         chosen = slice(row * comps, (row + 1) * comps)
         outs[1][chosen, :] = jnp.where(even, planes[-1], planes[0])
-        if with_spare:
-            outs[2][chosen, :] = jnp.where(even, planes[0], planes[-1])
+        outs[2][chosen, :] = jnp.where(even, planes[0], planes[-1])
     for ref in outs[1:]:
         ref[TILE * comps :, :] = correlation_ref[...]
 
@@ -311,25 +353,26 @@
         functools.partial(step_kernel, spare),
         name="step_rows",
         in_specs=[SCALARS] + [WHOLE] * (5 + len(sums)),
-        out_specs=[WHOLE] * (2 + spare),
-        out_shape=[jax.ShapeDtypeStruct(base.shape, jnp.float32), edge] + [edge] * spare,
-        compiler_params=pltpu.CompilerParams(vmem_limit_bytes=12 << 20),
+        out_specs=[WHOLE] * 3,
+        out_shape=[jax.ShapeDtypeStruct(base.shape, jnp.float32), edge, edge],
+        compiler_params=pltpu.CompilerParams(vmem_limit_bytes=6 << 20),
     )(where, *prepared, correlation, *sums)
 
 
 def diffuse_kernel(
     where_ref,
-    support_ref,
+    more_ref,
+    act_ref,
     correlation_ref,
     field_ref,
     inner_ref,
     outer_ref,
+    again_ref,
     out_ref,
     done_ref,
     edge_ref,
     weight_ref,
     keep_ref,
-    mask_ref,
     sent,
 ):
     rows, comps, cols = field_ref.shape
@@ -338,11 +381,13 @@
     group = GROUP
     index, last = where_ref[0], where_ref[2]
     odd = lax.rem(index, 2) == 1
+    again = more_ref[0] > 0
     has_above = jnp.where(index > 0, 1.0, 0.0)
     has_below = jnp.where(index < last, 1.0, 0.0)
     for row in range(PASSES):
         chosen = slice(row * comps, (row + 1) * comps)
-        inner, outer = inner_ref[chosen, :], outer_ref[chosen, :]
+        inner = inner_ref[chosen, :]
+        outer = jnp.where(again, again_ref[chosen, :], outer_ref[chosen, :])
         edge_ref[row] = has_above * jnp.where(odd, inner, outer)
         edge_ref[PASSES + row] = has_below * jnp.where(odd, outer, inner)
     inner, outer = inner_ref[PASSES * comps :, :], outer_ref[PASSES * comps :, :]
@@ -356,10 +401,6 @@
             line = jnp.broadcast_to(weight[row : row + 1, :], (GROUP, cols))
             weight_ref[first + row] = line
             keep_ref[first + row] = 1.0 - 4.0 * line
-    support = support_ref[...]
-    for tile in range(tiles):
-        act = active(support, index * tiles + tile, 1)
-        mask_ref[tile] = jnp.broadcast_to(act, mask_ref.shape[1:])
     lane = iota((group, LANES), 1)
     at_left, at_right = lane == 0, lane == LANES - 1
     nothing = jnp.zeros((group, LANES), jnp.float32)
@@ -372,7 +413,6 @@
 
     def relax(step, carry):
         start = pl.multiple_of(step * group, group)
-        planes = [{} for _ in range(PASSES + 1)]
 
         def load(row):
             if row < PASSES:
@@ -383,8 +423,9 @@
                 ref, at = edge_ref, row - rows
             return [ref[at, pl.ds(start, group), piece * LANES : (piece + 1) * LANES] for piece in range(pieces)]
 
-        def renew(done, row):
-            above, center, below = (planes[done][row + shift] for shift in (-1, 0, 1))
+        def renew(planes, done, at):
+            above, center, below = planes[at - 1 : at + 2]
+            row = at + done
             to_right = [pltpu.roll(piece, 1, 1) for piece in center]
             to_left = [pltpu.roll(piece, LANES - 1, 1) for piece in center]
             fresh = []
@@ -396,20 +437,14 @@
                 fresh.append(keep_ref[row, :, lanes] * center[piece] + weight_ref[row, :, lanes] * beside)
             return fresh
 
-        masks = [mask_ref[tile, pl.ds(start, group), :] for tile in range(tiles)]
-        for front in range(total + PASSES):
-            if front < total:
-                planes[0][front] = load(front)
-            for done in range(PASSES):
-                row = front - 1 - done
-                if done < row < total - 1 - done:
-                    planes[done + 1][row] = renew(done, row)
-                    planes[done].pop(row - 1)
-                    if done == PASSES - 1:
-                        own = row - PASSES
-                        for piece in range(pieces):
-                            at = pl.ds(step * size + piece * rows + own, group, stride=rows * pieces)
-                            done_ref[at, :] = planes[PASSES][row][piece] * masks[own // TILE]
+        masks = [act_ref[tile, pl.ds(start, group), :] for tile in range(tiles)]
+        planes = [load(row) for row in range(total)]
+        for done in range(PASSES):
+            planes = [renew(planes, done, at) for at in range(1, len(planes) - 1)]
+        for own in range(rows):
+            for piece in range(pieces):
+                at = pl.ds(step * size + piece * rows + own, group, stride=rows * pieces)
+                done_ref[at, :] = planes[own][piece] * masks[own // TILE]
         copy(step).start()
         return carry
 
@@ -418,7 +453,7 @@
         copy(step).wait()
 
 
-def diffuse(where, support, correlation, field, inner, outer):
+def diffuse(where, more, act, correlation, field, inner, outer, outer_again):
     rows, comps, cols = field.shape
     pieces = cols // LANES
     lines = VMEM((rows + 2 * PASSES, GROUP, cols), jnp.float32)
@@ -426,7 +461,7 @@
     return pl.pallas_call(
         diffuse_kernel,
         name="diffuse",
-        in_specs=[SCALARS] + [WHOLE] * 5,
+        in_specs=[SCALARS] * 2 + [WHOLE] * 6,
         out_specs=pl.BlockSpec(memory_space=pltpu.HBM),
         out_shape=jax.ShapeDtypeStruct(shape, jnp.float32),
         scratch_shapes=[
@@ -434,11 +469,10 @@
             VMEM((2 * PASSES, comps, cols), jnp.float32),
             lines,
             lines,
-            VMEM((rows // TILE, comps, LANES), jnp.float32),
             pltpu.SemaphoreType.DMA((comps // GROUP,)),
         ],
-        compiler_params=pltpu.CompilerParams(vmem_limit_bytes=16 << 20),
-    )(where, support, correlation, field, inner, outer)
+        compiler_params=pltpu.CompilerParams(vmem_limit_bytes=8 << 20),
+    )(where, more, act, correlation, field, inner, outer, outer_again)
 
 
 def pairs_of(count, first):
@@ -482,10 +516,12 @@
     mine[0], other[0] = project(where, names, traces, recording, 0, CHUNKS[:1])
     *_, later = barrier(other[0], traces)
     mine[1], other[1] = project(where, names, later, recording, CHUNKS[0], CHUNKS[1:])
+    *_, later = barrier(other[0], field_tiles)
+    planes, act, first, pick, late, more = plan(where, support, later, rows, count)
     if line:
         first_received = near(other[0])
         half = [barrier(mine[0] + first_received)[0]]
-        later, half[0] = barrier(other[1], half[0])
+        later, half[0], planes = barrier(other[1], half[0], planes)
         first_across = far(half[0])
         half.append(barrier(mine[1] + near(later))[0])
         whole = [barrier(half[0] + first_across)[0]]
@@ -496,9 +532,11 @@
     else:
         whole, back = lax.psum((mine, other), "tm")
     sums = [barrier(in_order(odd, *barrier(whole[0], back[0])))[0]]
-    *prepared, to_outer, more = prepare(where, support, sums[0], field_tiles, correlation, count)
+    to_outer = edge_rows(where, sums[0], planes, act, first, correlation)
     outer = beside(to_outer)
-    own, theirs, *prepared = barrier(whole[1], back[1], *prepared)
+    *_, later = barrier(to_outer, planes)
+    own, theirs, base, rate = barrier(whole[1], back[1], *prepare(sums[0], later, act))
+    prepared = base, pick, late, rate
     sums.append(barrier(in_order(odd, own, theirs))[0])
 
     def rest():
@@ -510,15 +548,15 @@
         else:
             mine, other = lax.psum((mine, other), "tm")
         field, to_inner, to_outer = step_rows(where, prepared, correlation, sums + [in_order(odd, mine, other)])
-        return field, to_inner, beside(to_outer)
+        return field, to_inner, jnp.maximum(beside(to_outer), 0.0)
 
     def enough():
-        field, to_inner = step_rows(where, prepared, correlation, sums)
-        return field, to_inner, outer
-
-    field, to_inner, outer = lax.cond(more[0] > 0, rest, enough)
+        return tuple(step_rows(where, prepared, correlation, sums))
+
+    field, to_inner, outer_again = lax.cond(more[0] > 0, rest, enough)
+    to_inner, outer = barrier(to_inner, outer)
     inner = lax.ppermute(to_inner, "rows", inside)
-    result = diffuse(where, support, correlation, field, inner, outer)
+    result = diffuse(where, more, act, correlation, field, inner, outer, outer_again)
     return from_tiles(result, comps, rows, cols)
 
 

time: 56.6 us -> 54 us (0.954)
  waiting for transfers between devices: 24.6 us -> 18.8 us
  starting transfers between devices: 11 us -> 13.2 us
  Pallas kernels: 19.6 us -> 20.5 us
    ppermute x4, waiting for transfers between devices: 20.6 us -> 15.1 us  [near(): return lax.ppermute(array, 'tm', NEAR)]
    ppermute x2, starting transfers between devices: 3.42 us -> 4.72 us  [far(): return lax.ppermute(array, 'tm', FAR)]
    ppermute x1, starting transfers between devices: 4.32 us -> 5.2 us  [beside(): return lax.ppermute(array, 'rows', outside)]
    pallas_call x2 -> x4, Pallas kernels: 9.75 us -> 10.2 us  [the longest x1 5.91 us: diffuse(): pl.pallas_call(diffuse_kernel, name='diffuse', in_specs=[SCALARS] * 2 + [...]
  transfers between devices with their start and end apart: 8 -> 8, of which waited for: 6 -> 5; matrix products, arithmetic and copies ran while one was open for 0% -> 0% of each run, Pallas kernels for 10% -> 18%
where the time goes in v3:
time: 54 us; the launch traced here: 53.7 us
  Pallas kernels  20.5 us (38%)
  waiting for transfers between devices  18.8 us (35%)
  starting transfers between devices  13.2 us (24%)
  between operations  0.87 us (2%)
    ppermute x4, waiting for transfers between devices, near(): return lax.ppermute(array, 'tm', NEAR)  15.1 us
    pallas_call x2, Pallas kernels, project(): pl.pallas_call(functools.partial(project_kernel, first, chunks), name='pr...  9.41 us
    pallas_call x1, Pallas kernels, diffuse(): pl.pallas_call(diffuse_kernel, name='diffuse', in_specs=[SCALARS] * 2 + [...  5.91 us
    ppermute x1, starting transfers between devices, beside(): return lax.ppermute(array, 'rows', outside)  5.2 us
    ppermute x2, starting transfers between devices, far(): return lax.ppermute(array, 'tm', FAR)  4.72 us
    ppermute x4, starting transfers between devices, near(): return lax.ppermute(array, 'tm', NEAR)  3.27 us
    pallas_call x1, Pallas kernels, plan(): pl.pallas_call(functools.partial(plan_kernel, count), name='plan', in_spe...  1.97 us
    ppermute x1, waiting for transfers between devices, per_device(): inner = lax.ppermute(to_inner, 'rows', inside)  1.93 us
  transfers between devices with their start and end apart: 8, of which 5 were waited for; matrix products, arithmetic and copies ran while one was open for 0% of the time, Pallas kernels for 18%

profile of v3, /device:TPU:1, one launch (start us, length us, event | category | flops | bytes accessed | tf_op | source)
XLA Modules:
  0.0 53.7 jit_solution(9171107715460578604)
XLA Ops:
  0.0 0.0 copy-start.1
  0.0 0.0 copy-start.3
  0.0 0.1 pad_add_fusion.where_ref
  0.1 0.0 copy-start
  0.1 4.9 %project.4 = (f32[104,512]{1,0:T(8,128)S(1)}, f32[104,512]{1,0:T(8,128)S(1)}) custom-call(s32[3]{0:T(128)S(1)} %pad_add_fusion.where_ref, s32[4,64]{1,0:T(4,128)} %bitcast.20, bf16[64,1024]{1,0:T(8,128)(2,1)} %traces_ref.2, bf16[8192,512]{1,0:T(8,128)(2,1)} %bitcast.17), custom_call_target="tpu_custom_call" | custom-call | tf_op jit(solution)/shard_map/project/pallas_call | solution.py:129
  5.0 0.0 copy-start.2
  5.0 2.2 %collective-permute-start.4 = (f32[104,512]{1,0:T(8,128)S(1)}, f32[104,512]{1,0:T(8,128)S(1)}, u32[]{:S(2)}, u32[]{:S(2)}) collective-permute-start(f32[104,512]{1,0:T(8,128)S(1)} %get-tuple-element.101), channel_id=1, source_target_pairs={{0,4},{4,0},{8,12},{12,8},{1,5},{5,1},{9,13},{13,9},{2,6},{6,2},{1... | collective-permute-start | bytes 638984 | tf_op jit(solution)/shard_map/ppermute | solution.py:507
  7.2 0.0 copy-done.3
  7.2 0.1 copy.6.support_ref
  7.3 0.0 copy-done.1
  7.3 4.5 %project.5 = (f32[64,512]{1,0:T(8,128)S(1)}, f32[64,512]{1,0:T(8,128)S(1)}) custom-call(s32[3]{0:T(128)S(1)} %pad_add_fusion.where_ref, s32[4,64]{1,0:T(4,128)S(1)} %bitcast.21, bf16[64,1024]{1,0:T(8,128)(2,1)S(1)} %copy-done.1, bf16[8192,512]{1,0:T(8,128)(2,1)} %bitcast.18), custom_call_target="tpu_custom_call" | custom-call | tf_op jit(solution)/shard_map/project/pallas_call | solution.py:129
  11.8 0.0 copy-done
  11.8 2.0 %plan.1 = (f32[8,64,512]{2,1,0:T(8,128)S(1)}, f32[2,64,128]{2,1,0:T(8,128)S(1)}, bf16[64,256]{1,0:T(8,128)(2,1)S(1)}, bf16[128,256]{1,0:T(8,128)(2,1)S(1)}, bf16[128,256]{1,0:T(8,128)(2,1)S(1)}, /*index=5*/s32[1]{0:T(128)}) custom-call(s32[3]{0:T(128)S(1)} %pad_add_fusion.where_ref, s32[64,4]{1,0:T(8,128)S(1)} %copy.6.support_ref, f32[2048,128]{1,0:T(8,128)S(1)} %bitcast.16), custom_call_target="tpu_custom_call" | custom-call | tf_op jit(solution)/shard_map/plan/pallas_call | solution.py:258
  13.8 0.0 collective-permute-done.4
  13.8 2.3 %collective-permute-start.6 = (f32[104,512]{1,0:T(8,128)S(1)}, f32[104,512]{1,0:T(8,128)S(1)}, u32[]{:S(2)}, u32[]{:S(2)}) collective-permute-start(f32[104,512]{1,0:T(8,128)S(1)} %add.18), channel_id=1, source_target_pairs={{0,12},{4,8},{8,4},{12,0},{1,13},{5,9},{9,5},{13,1},{2,14},{6,10},... | collective-permute-start | bytes 638984 | tf_op jit(solution)/shard_map/ppermute | solution.py:510
  16.1 0.4 collective-permute-start.5
  16.5 9.3 %collective-permute-done.5 = f32[64,512]{1,0:T(8,128)S(1)} collective-permute-done((f32[64,512]{1,0:T(8,128)S(1)}, f32[64,512]{1,0:T(8,128)S(1)}, u32[]{:S(2)}, u32[]{:S(2)}) %collective-permute-start.5) | collective-permute-done | bytes 131104 | tf_op jit(solution)/shard_map/ppermute | solution.py:507
  25.8 0.0 collective-permute-done.6
  25.9 0.1 collective-permute-start.9
  25.9 2.5 %collective-permute-start.7 = (f32[64,512]{1,0:T(8,128)S(1)}, f32[64,512]{1,0:T(8,128)S(1)}, u32[]{:S(2)}, u32[]{:S(2)}) collective-permute-start(f32[64,512]{1,0:T(8,128)S(1)} %add.19), channel_id=1, source_target_pairs={{0,12},{4,8},{8,4},{12,0},{1,13},{5,9},{9,5},{13,1},{2,14},{6,10},... | collective-permute-start | bytes 393224 | tf_op jit(solution)/shard_map/ppermute | solution.py:510
  28.4 3.9 %collective-permute-done.9 = f32[104,512]{1,0:T(8,128)S(1)} collective-permute-done((f32[104,512]{1,0:T(8,128)S(1)}, f32[104,512]{1,0:T(8,128)S(1)}, u32[]{:S(2)}, u32[]{:S(2)}) %collective-permute-start.9) | collective-permute-done | bytes 213024 | tf_op jit(solution)/shard_map/ppermute | solution.py:507
  32.3 0.0 copy-done.2
  32.3 1.3 %edge_rows.1 = f32[264,512]{1,0:T(8,128)S(1)} custom-call(s32[3]{0:T(128)S(1)} %pad_add_fusion.where_ref, f32[208,512]{1,0:T(8,128)S(1)} %pad_maximum_fusion.1.sums_ref, f32[8,64,512]{2,1,0:T(8,128)S(1)} %get-tuple-element.118.planes_ref, f32[2,64,128]{2,1,0:T(8,128)S(1)} %get-tuple-element.104.act_ref, bf16[64,256]{1,0:T(8,128)(2,1)S(1)} %get-tuple-element.117.first_ref, ...), custom_call_target="tpu_custom_call" | custom-call | tf_op jit(solution)/shard_map/edge_rows/pallas_call | solution.py:290
  33.6 5.2 %collective-permute-start.10 = (f32[264,512]{1,0:T(8,128)S(1)}, f32[264,512]{1,0:T(8,128)S(1)}, u32[]{:S(2)}, u32[]{:S(2)}) collective-permute-start(f32[264,512]{1,0:T(8,128)S(1)} %edge_rows.1), channel_id=1, source_target_pairs={{0,0},{1,2},{2,1},{3,3},{4,4},{5,6},{6,5},{7,7},{8,8},{9,10},{10,9... | collective-permute-start | bytes 1622024 | tf_op jit(solution)/shard_map/ppermute | solution.py:513
  38.8 0.0 collective-permute-done.7
  38.9 0.6 %collective-permute-start.8 = (f32[64,512]{1,0:T(8,128)S(1)}, f32[64,512]{1,0:T(8,128)S(1)}, u32[]{:S(2)}, u32[]{:S(2)}) collective-permute-start(f32[64,512]{1,0:T(8,128)S(1)} %add.21), channel_id=1, source_target_pairs={{0,4},{4,0},{8,12},{12,8},{1,5},{5,1},{9,13},{13,9},{2,6},{6,2},{1... | collective-permute-start | bytes 393224 | tf_op jit(solution)/shard_map/ppermute | solution.py:507
  40.2 1.0 %prepare.1 = (f32[8,64,512]{2,1,0:T(8,128)S(1)}, f32[64,128]{1,0:T(8,128)S(1)}) custom-call(f32[208,512]{1,0:T(8,128)S(1)} %pad_maximum_fusion.1.sums_ref, f32[8,64,512]{2,1,0:T(8,128)S(1)} %get-tuple-element.118.planes_ref, f32[2,64,128]{2,1,0:T(8,128)S(1)} %get-tuple-element.104.act_ref), custom_call_target="tpu_custom_call" | custom-call | tf_op jit(solution)/shard_map/prepare/pallas_call | solution.py:309
  41.2 2.0 %collective-permute-done.8 = f32[64,512]{1,0:T(8,128)S(1)} collective-permute-done((f32[64,512]{1,0:T(8,128)S(1)}, f32[64,512]{1,0:T(8,128)S(1)}, u32[]{:S(2)}, u32[]{:S(2)}) %collective-permute-start.8) | collective-permute-done | bytes 131104 | tf_op jit(solution)/shard_map/ppermute | solution.py:507
  43.2 0.9 %conditional.1 = ((f32[8,64,512]{2,1,0:T(8,128)S(1)}, f32[264,512]{1,0:T(8,128)S(1)}, f32[264,512]{1,0:T(8,128)S(1)})) conditional(s32[]{:T(128)} %bitcast.8, (s32[3]{0:T(128)S(1)}, f32[8,64,512]{2,1,0:T(8,128)S(1)}, bf16[128,256]{1,0:T(8,128)(2,1)S(1)}, bf16[128,256]{1,0:T(8,128)(2,1)S(1)}, f32[64,128]{1,0:T(8,128)S(1)}, ...), branch_computations={%region_0.1_spmd, %region_1.2_spmd} | conditional | flops 430080 | bytes 8356033 | solution.py:556
  43.2 0.9 %step_rows.2 = (f32[8,64,512]{2,1,0:T(8,128)S(1)}, f32[264,512]{1,0:T(8,128)S(1)}, f32[264,512]{1,0:T(8,128)S(1)}) custom-call(s32[3]{0:T(128)S(1)} %get-tuple-element.45.where_ref, f32[8,64,512]{2,1,0:T(8,128)S(1)} %get-tuple-element.46.base_ref, bf16[128,256]{1,0:T(8,128)(2,1)S(1)} %get-tuple-element.47.pick_ref, ...), custom_call_target="tpu_custom_call" | custom-call | tf_op jit(solution)/shard_map/cond/branch_0_fun/step_rows/pallas_call | solution.py:352
  44.1 1.7 %collective-permute-done.10.outer_ref = f32[264,512]{1,0:T(8,128)S(1)} collective-permute-done((f32[264,512]{1,0:T(8,128)S(1)}, f32[264,512]{1,0:T(8,128)S(1)}, u32[]{:S(2)}, u32[]{:S(2)}) %collective-permute-start.10) | collective-permute-done | bytes 540704 | tf_op jit(solution)/shard_map/ppermute | solution.py:513
  45.9 0.0 collective-permute-start.11
  45.9 1.9 %collective-permute-done.11.inner_ref = f32[264,512]{1,0:T(8,128)S(1)} collective-permute-done((f32[264,512]{1,0:T(8,128)S(1)}, f32[264,512]{1,0:T(8,128)S(1)}, u32[]{:S(2)}, u32[]{:S(2)}) %collective-permute-start.11) | collective-permute-done | bytes 540704 | tf_op jit(solution)/shard_map/ppermute | solution.py:558
  47.8 5.9 %diffuse.1 = f32[2048,128]{1,0:T(8,128)} custom-call(s32[3]{0:T(128)S(1)} %pad_add_fusion.where_ref, s32[1]{0:T(128)} %get-tuple-element.103.more_ref, f32[2,64,128]{2,1,0:T(8,128)S(1)} %get-tuple-element.104.act_ref, f32[8,512]{1,0:T(8,128)S(1)} %copy-done.2, f32[8,64,512]{2,1,0:T(8,128)S(1)} %get-tuple-element.127.field_ref, ...), custom_call_target="tpu_custom_call" | custom-call | tf_op jit(solution)/shard_map/diffuse/pallas_call | solution.py:461
  (8 shorter events, 0.2 us)
Async XLA Ops:
  0.0 7.3 %copy-start.1 = (bf16[64,1024]{1,0:T(8,128)(2,1)S(1)}, bf16[64,1024]{1,0:T(8,128)(2,1)}, u32[]{:S(2)}) copy-start(bf16[64,1024]{1,0:T(8,128)(2,1)} %traces_ref.2) | copy-start | bytes 393220
  0.0 7.2 %copy-start.3 = (s32[64,4]{0,1:T(4,128)S(1)}, s32[64,4]{0,1:T(4,128)}, u32[]{:S(2)}) copy-start(s32[64,4]{0,1:T(4,128)} %param.11) | copy-start | bytes 3076
  0.1 11.7 %copy-start = (f32[64,8,512]{2,1,0:T(8,128)S(1)}, f32[64,8,512]{2,1,0:T(8,128)}, u32[]{:S(2)}) copy-start(f32[64,8,512]{2,1,0:T(8,128)} %param.9) | copy-start | bytes 3145732
  5.0 27.3 %copy-start.2 = (f32[8,512]{1,0:T(8,128)S(1)}, f32[8,512]{1,0:T(8,128)}, u32[]{:S(2)}) copy-start(f32[8,512]{1,0:T(8,128)} %correlation_ref.3) | copy-start | bytes 49156
  5.0 8.8 %collective-permute-start.4 = (f32[104,512]{1,0:T(8,128)S(1)}, f32[104,512]{1,0:T(8,128)S(1)}, u32[]{:S(2)}, u32[]{:S(2)}) collective-permute-start(f32[104,512]{1,0:T(8,128)S(1)} %get-tuple-element.101), channel_id=1, source_target_pairs={{0,4},{4,0},{8,12},{12,8},{1,5},{5,1},{9,13},{13,9},{2,6},{6,2},{1... | collective-permute-start | bytes 638984 | tf_op jit(solution)/shard_map/ppermute | solution.py:507
  13.8 12.0 %collective-permute-start.6 = (f32[104,512]{1,0:T(8,128)S(1)}, f32[104,512]{1,0:T(8,128)S(1)}, u32[]{:S(2)}, u32[]{:S(2)}) collective-permute-start(f32[104,512]{1,0:T(8,128)S(1)} %add.18), channel_id=1, source_target_pairs={{0,12},{4,8},{8,4},{12,0},{1,13},{5,9},{9,5},{13,1},{2,14},{6,10},... | collective-permute-start | bytes 638984 | tf_op jit(solution)/shard_map/ppermute | solution.py:510
  16.1 9.7 %collective-permute-start.5 = (f32[64,512]{1,0:T(8,128)S(1)}, f32[64,512]{1,0:T(8,128)S(1)}, u32[]{:S(2)}, u32[]{:S(2)}) collective-permute-start(f32[64,512]{1,0:T(8,128)S(1)} %get-tuple-element.110), channel_id=1, source_target_pairs={{0,4},{4,0},{8,12},{12,8},{1,5},{5,1},{9,13},{13,9},{2,6},{6,2},{1... | collective-permute-start | bytes 393224 | tf_op jit(solution)/shard_map/ppermute | solution.py:507
  25.9 6.4 %collective-permute-start.9 = (f32[104,512]{1,0:T(8,128)S(1)}, f32[104,512]{1,0:T(8,128)S(1)}, u32[]{:S(2)}, u32[]{:S(2)}) collective-permute-start(f32[104,512]{1,0:T(8,128)S(1)} %add.20), channel_id=1, source_target_pairs={{0,4},{4,0},{8,12},{12,8},{1,5},{5,1},{9,13},{13,9},{2,6},{6,2},{1... | collective-permute-start | bytes 638984 | tf_op jit(solution)/shard_map/ppermute | solution.py:507
  25.9 12.9 %collective-permute-start.7 = (f32[64,512]{1,0:T(8,128)S(1)}, f32[64,512]{1,0:T(8,128)S(1)}, u32[]{:S(2)}, u32[]{:S(2)}) collective-permute-start(f32[64,512]{1,0:T(8,128)S(1)} %add.19), channel_id=1, source_target_pairs={{0,12},{4,8},{8,4},{12,0},{1,13},{5,9},{9,5},{13,1},{2,14},{6,10},... | collective-permute-start | bytes 393224 | tf_op jit(solution)/shard_map/ppermute | solution.py:510
  33.6 12.2 %collective-permute-start.10 = (f32[264,512]{1,0:T(8,128)S(1)}, f32[264,512]{1,0:T(8,128)S(1)}, u32[]{:S(2)}, u32[]{:S(2)}) collective-permute-start(f32[264,512]{1,0:T(8,128)S(1)} %edge_rows.1), channel_id=1, source_target_pairs={{0,0},{1,2},{2,1},{3,3},{4,4},{5,6},{6,5},{7,7},{8,8},{9,10},{10,9... | collective-permute-start | bytes 1622024 | tf_op jit(solution)/shard_map/ppermute | solution.py:513
  38.9 4.3 %collective-permute-start.8 = (f32[64,512]{1,0:T(8,128)S(1)}, f32[64,512]{1,0:T(8,128)S(1)}, u32[]{:S(2)}, u32[]{:S(2)}) collective-permute-start(f32[64,512]{1,0:T(8,128)S(1)} %add.21), channel_id=1, source_target_pairs={{0,4},{4,0},{8,12},{12,8},{1,5},{5,1},{9,13},{13,9},{2,6},{6,2},{1... | collective-permute-start | bytes 393224 | tf_op jit(solution)/shard_map/ppermute | solution.py:507
  45.9 1.9 %collective-permute-start.11 = (f32[264,512]{1,0:T(8,128)S(1)}, f32[264,512]{1,0:T(8,128)S(1)}, u32[]{:S(2)}, u32[]{:S(2)}) collective-permute-start(f32[264,512]{1,0:T(8,128)S(1)} %get-tuple-element.129), channel_id=1, source_target_pairs={{0,1},{1,0},{2,3},{3,2},{4,5},{5,4},{6,7},{7,6},{8,9},{9,8},{10,11... | collective-permute-start | bytes 1622024 | tf_op jit(solution)/shard_map/ppermute | solution.py:558

commit v4 on v3

--- a/solution.py
+++ b/solution.py
@@ -514,16 +514,17 @@
 
     mine, other = [None, None], [None, None]
     mine[0], other[0] = project(where, names, traces, recording, 0, CHUNKS[:1])
-    *_, later = barrier(other[0], traces)
-    mine[1], other[1] = project(where, names, later, recording, CHUNKS[0], CHUNKS[1:])
+    if not line:
+        mine[1], other[1] = project(where, names, traces, recording, CHUNKS[0], CHUNKS[1:])
     *_, later = barrier(other[0], field_tiles)
     planes, act, first, pick, late, more = plan(where, support, later, rows, count)
     if line:
         first_received = near(other[0])
-        half = [barrier(mine[0] + first_received)[0]]
-        later, half[0], planes = barrier(other[1], half[0], planes)
+        half = [barrier(mine[0] + first_received, planes)[0]]
         first_across = far(half[0])
-        half.append(barrier(mine[1] + near(later))[0])
+        *_, later = barrier(half[0], traces)
+        mine[1], other[1] = project(where, names, later, recording, CHUNKS[0], CHUNKS[1:])
+        half.append(barrier(mine[1] + near(other[1]))[0])
         whole = [barrier(half[0] + first_across)[0]]
         half[1], whole[0] = barrier(half[1], whole[0])
         first_back = near(whole[0])
@@ -548,7 +549,7 @@
         else:
             mine, other = lax.psum((mine, other), "tm")
         field, to_inner, to_outer = step_rows(where, prepared, correlation, sums + [in_order(odd, mine, other)])
-        return field, to_inner, jnp.maximum(beside(to_outer), 0.0)
+        return tuple(jnp.maximum(array, 0.0) for array in (field, to_inner, beside(to_outer)))
 
     def enough():
         return tuple(step_rows(where, prepared, correlation, sums))

time: 54 us -> 53.3 us (0.987)
  waiting for transfers between devices: 18.8 us -> 13.4 us
  starting transfers between devices: 13.2 us -> 17.4 us
    ppermute x4, waiting for transfers between devices: 15.1 us -> 9.91 us  [near(): return lax.ppermute(array, 'tm', NEAR)]
    ppermute x1, starting transfers between devices: 5.2 us -> 7.65 us  [beside(): return lax.ppermute(array, 'rows', outside)]
    ppermute x2, starting transfers between devices: 4.72 us -> 6.41 us  [far(): return lax.ppermute(array, 'tm', FAR)]
  transfers between devices with their start and end apart: 8 -> 8, of which waited for: 5 -> 6; matrix products, arithmetic and copies ran while one was open for 0% -> 0% of each run, Pallas kernels for 18% -> 18%
where the time goes in v4:
time: 53.3 us; the launch traced here: 52.6 us
  Pallas kernels  20.5 us (38%)
  starting transfers between devices  17.4 us (33%)
  waiting for transfers between devices  13.4 us (25%)
  between operations  0.86 us (2%)
    ppermute x4, waiting for transfers between devices, near(): return lax.ppermute(array, 'tm', NEAR)  9.91 us
    pallas_call x2, Pallas kernels, project(): pl.pallas_call(functools.partial(project_kernel, first, chunks), name='pr...  9.42 us
    ppermute x1, starting transfers between devices, beside(): return lax.ppermute(array, 'rows', outside)  7.65 us
    ppermute x2, starting transfers between devices, far(): return lax.ppermute(array, 'tm', FAR)  6.41 us
    pallas_call x1, Pallas kernels, diffuse(): pl.pallas_call(diffuse_kernel, name='diffuse', in_specs=[SCALARS] * 2 + [...  5.91 us
    ppermute x4, starting transfers between devices, near(): return lax.ppermute(array, 'tm', NEAR)  3.37 us
    pallas_call x1, Pallas kernels, plan(): pl.pallas_call(functools.partial(plan_kernel, count), name='plan', in_spe...  1.97 us
    ppermute x1, waiting for transfers between devices, per_device(): inner = lax.ppermute(to_inner, 'rows', inside)  1.93 us
  transfers between devices with their start and end apart: 8, of which 6 were waited for; matrix products, arithmetic and copies ran while one was open for 0% of the time, Pallas kernels for 18%

profile of v4, /device:TPU:1, one launch (start us, length us, event | category | flops | bytes accessed | tf_op | source)
XLA Modules:
  0.0 52.6 jit_solution(5634851967200678275)
XLA Ops:
  0.0 0.0 copy-start.1
  0.0 0.0 copy-start.3
  0.0 0.0 copy-start
  0.0 0.1 pad_add_fusion.where_ref
  0.1 4.9 %project.4 = (f32[104,512]{1,0:T(8,128)S(1)}, f32[104,512]{1,0:T(8,128)S(1)}) custom-call(s32[3]{0:T(128)S(1)} %pad_add_fusion.where_ref, s32[4,64]{1,0:T(4,128)} %bitcast.20, bf16[64,1024]{1,0:T(8,128)(2,1)} %traces_ref.2, bf16[8192,512]{1,0:T(8,128)(2,1)} %bitcast.17), custom_call_target="tpu_custom_call" | custom-call | tf_op jit(solution)/shard_map/project/pallas_call | solution.py:129
  5.0 0.0 copy-start.2
  5.1 2.2 %collective-permute-start.4 = (f32[104,512]{1,0:T(8,128)S(1)}, f32[104,512]{1,0:T(8,128)S(1)}, u32[]{:S(2)}, u32[]{:S(2)}) collective-permute-start(f32[104,512]{1,0:T(8,128)S(1)} %get-tuple-element.99), channel_id=1, source_target_pairs={{0,4},{4,0},{8,12},{12,8},{1,5},{5,1},{9,13},{13,9},{2,6},{6,2},{1... | collective-permute-start | bytes 638984 | tf_op jit(solution)/shard_map/ppermute | solution.py:507
  7.2 0.0 copy-done.3
  7.2 0.1 copy.6.support_ref
  7.3 0.0 copy-done
  7.3 2.0 %plan.1 = (f32[8,64,512]{2,1,0:T(8,128)S(1)}, f32[2,64,128]{2,1,0:T(8,128)S(1)}, bf16[64,256]{1,0:T(8,128)(2,1)S(1)}, bf16[128,256]{1,0:T(8,128)(2,1)S(1)}, bf16[128,256]{1,0:T(8,128)(2,1)S(1)}, /*index=5*/s32[1]{0:T(128)}) custom-call(s32[3]{0:T(128)S(1)} %pad_add_fusion.where_ref, s32[64,4]{1,0:T(8,128)S(1)} %copy.6.support_ref, f32[2048,128]{1,0:T(8,128)S(1)} %bitcast.16), custom_call_target="tpu_custom_call" | custom-call | tf_op jit(solution)/shard_map/plan/pallas_call | solution.py:258
  9.3 2.9 %collective-permute-done.4 = f32[104,512]{1,0:T(8,128)S(1)} collective-permute-done((f32[104,512]{1,0:T(8,128)S(1)}, f32[104,512]{1,0:T(8,128)S(1)}, u32[]{:S(2)}, u32[]{:S(2)}) %collective-permute-start.4) | collective-permute-done | bytes 213024 | tf_op jit(solution)/shard_map/ppermute | solution.py:507
  12.3 3.2 %collective-permute-start.6 = (f32[104,512]{1,0:T(8,128)S(1)}, f32[104,512]{1,0:T(8,128)S(1)}, u32[]{:S(2)}, u32[]{:S(2)}) collective-permute-start(f32[104,512]{1,0:T(8,128)S(1)} %add.18), channel_id=1, source_target_pairs={{0,12},{4,8},{8,4},{12,0},{1,13},{5,9},{9,5},{13,1},{2,14},{6,10},... | collective-permute-start | bytes 638984 | tf_op jit(solution)/shard_map/ppermute | solution.py:510
  15.5 0.0 copy-done.1
  15.5 4.5 %project.5 = (f32[64,512]{1,0:T(8,128)S(1)}, f32[64,512]{1,0:T(8,128)S(1)}) custom-call(s32[3]{0:T(128)S(1)} %pad_add_fusion.where_ref, s32[4,64]{1,0:T(4,128)S(1)} %bitcast.21, bf16[64,1024]{1,0:T(8,128)(2,1)S(1)} %copy-done.1, bf16[8192,512]{1,0:T(8,128)(2,1)} %bitcast.18), custom_call_target="tpu_custom_call" | custom-call | tf_op jit(solution)/shard_map/project/pallas_call | solution.py:129
  20.0 0.1 collective-permute-start.5
  20.1 3.8 %collective-permute-done.5 = f32[64,512]{1,0:T(8,128)S(1)} collective-permute-done((f32[64,512]{1,0:T(8,128)S(1)}, f32[64,512]{1,0:T(8,128)S(1)}, u32[]{:S(2)}, u32[]{:S(2)}) %collective-permute-start.5) | collective-permute-done | bytes 131104 | tf_op jit(solution)/shard_map/ppermute | solution.py:507
  23.9 0.0 collective-permute-done.6
  23.9 0.4 collective-permute-start.9
  24.4 3.2 %collective-permute-start.7 = (f32[64,512]{1,0:T(8,128)S(1)}, f32[64,512]{1,0:T(8,128)S(1)}, u32[]{:S(2)}, u32[]{:S(2)}) collective-permute-start(f32[64,512]{1,0:T(8,128)S(1)} %add.19), channel_id=1, source_target_pairs={{0,12},{4,8},{8,4},{12,0},{1,13},{5,9},{9,5},{13,1},{2,14},{6,10},... | collective-permute-start | bytes 393224 | tf_op jit(solution)/shard_map/ppermute | solution.py:510
  27.5 1.2 %collective-permute-done.9 = f32[104,512]{1,0:T(8,128)S(1)} collective-permute-done((f32[104,512]{1,0:T(8,128)S(1)}, f32[104,512]{1,0:T(8,128)S(1)}, u32[]{:S(2)}, u32[]{:S(2)}) %collective-permute-start.9) | collective-permute-done | bytes 213024 | tf_op jit(solution)/shard_map/ppermute | solution.py:507
  28.8 0.0 copy-done.2
  28.8 1.3 %edge_rows.1 = f32[264,512]{1,0:T(8,128)S(1)} custom-call(s32[3]{0:T(128)S(1)} %pad_add_fusion.where_ref, f32[208,512]{1,0:T(8,128)S(1)} %pad_maximum_fusion.1.sums_ref, f32[8,64,512]{2,1,0:T(8,128)S(1)} %get-tuple-element.114.planes_ref, f32[2,64,128]{2,1,0:T(8,128)S(1)} %get-tuple-element.102.act_ref, bf16[64,256]{1,0:T(8,128)(2,1)S(1)} %get-tuple-element.113.first_ref, ...), custom_call_target="tpu_custom_call" | custom-call | tf_op jit(solution)/shard_map/edge_rows/pallas_call | solution.py:290
  30.1 7.6 %collective-permute-start.10 = (f32[264,512]{1,0:T(8,128)S(1)}, f32[264,512]{1,0:T(8,128)S(1)}, u32[]{:S(2)}, u32[]{:S(2)}) collective-permute-start(f32[264,512]{1,0:T(8,128)S(1)} %edge_rows.1), channel_id=1, source_target_pairs={{0,0},{1,2},{2,1},{3,3},{4,4},{5,6},{6,5},{7,7},{8,8},{9,10},{10,9... | collective-permute-start | bytes 1622024 | tf_op jit(solution)/shard_map/ppermute | solution.py:513
  37.7 0.0 collective-permute-done.7
  37.7 0.7 %collective-permute-start.8 = (f32[64,512]{1,0:T(8,128)S(1)}, f32[64,512]{1,0:T(8,128)S(1)}, u32[]{:S(2)}, u32[]{:S(2)}) collective-permute-start(f32[64,512]{1,0:T(8,128)S(1)} %add.21), channel_id=1, source_target_pairs={{0,4},{4,0},{8,12},{12,8},{1,5},{5,1},{9,13},{13,9},{2,6},{6,2},{1... | collective-permute-start | bytes 393224 | tf_op jit(solution)/shard_map/ppermute | solution.py:507
  39.1 1.0 %prepare.1 = (f32[8,64,512]{2,1,0:T(8,128)S(1)}, f32[64,128]{1,0:T(8,128)S(1)}) custom-call(f32[208,512]{1,0:T(8,128)S(1)} %pad_maximum_fusion.1.sums_ref, f32[8,64,512]{2,1,0:T(8,128)S(1)} %get-tuple-element.114.planes_ref, f32[2,64,128]{2,1,0:T(8,128)S(1)} %get-tuple-element.102.act_ref), custom_call_target="tpu_custom_call" | custom-call | tf_op jit(solution)/shard_map/prepare/pallas_call | solution.py:309
  40.2 2.0 %collective-permute-done.8 = f32[64,512]{1,0:T(8,128)S(1)} collective-permute-done((f32[64,512]{1,0:T(8,128)S(1)}, f32[64,512]{1,0:T(8,128)S(1)}, u32[]{:S(2)}, u32[]{:S(2)}) %collective-permute-start.8) | collective-permute-done | bytes 131104 | tf_op jit(solution)/shard_map/ppermute | solution.py:507
  42.3 0.9 %conditional.1 = ((f32[8,64,512]{2,1,0:T(8,128)S(1)}, f32[264,512]{1,0:T(8,128)S(1)}, f32[264,512]{1,0:T(8,128)S(1)})) conditional(s32[]{:T(128)} %bitcast.8, (s32[3]{0:T(128)S(1)}, f32[8,64,512]{2,1,0:T(8,128)S(1)}, bf16[128,256]{1,0:T(8,128)(2,1)S(1)}, bf16[128,256]{1,0:T(8,128)(2,1)S(1)}, f32[64,128]{1,0:T(8,128)S(1)}, ...), branch_computations={%region_0.1_spmd, %region_1.2_spmd} | conditional | flops 827392 | bytes 11534529 | solution.py:557
  42.3 0.9 %step_rows.2 = (f32[8,64,512]{2,1,0:T(8,128)S(1)}, f32[264,512]{1,0:T(8,128)S(1)}, f32[264,512]{1,0:T(8,128)S(1)}) custom-call(s32[3]{0:T(128)S(1)} %get-tuple-element.45.where_ref, f32[8,64,512]{2,1,0:T(8,128)S(1)} %get-tuple-element.46.base_ref, bf16[128,256]{1,0:T(8,128)(2,1)S(1)} %get-tuple-element.47.pick_ref, ...), custom_call_target="tpu_custom_call" | custom-call | tf_op jit(solution)/shard_map/cond/branch_0_fun/step_rows/pallas_call | solution.py:352
  43.2 1.5 %collective-permute-done.10.outer_ref = f32[264,512]{1,0:T(8,128)S(1)} collective-permute-done((f32[264,512]{1,0:T(8,128)S(1)}, f32[264,512]{1,0:T(8,128)S(1)}, u32[]{:S(2)}, u32[]{:S(2)}) %collective-permute-start.10) | collective-permute-done | bytes 540704 | tf_op jit(solution)/shard_map/ppermute | solution.py:513
  44.7 0.0 collective-permute-start.11
  44.7 1.9 %collective-permute-done.11.inner_ref = f32[264,512]{1,0:T(8,128)S(1)} collective-permute-done((f32[264,512]{1,0:T(8,128)S(1)}, f32[264,512]{1,0:T(8,128)S(1)}, u32[]{:S(2)}, u32[]{:S(2)}) %collective-permute-start.11) | collective-permute-done | bytes 540704 | tf_op jit(solution)/shard_map/ppermute | solution.py:559
  46.7 5.9 %diffuse.1 = f32[2048,128]{1,0:T(8,128)} custom-call(s32[3]{0:T(128)S(1)} %pad_add_fusion.where_ref, s32[1]{0:T(128)} %get-tuple-element.101.more_ref, f32[2,64,128]{2,1,0:T(8,128)S(1)} %get-tuple-element.102.act_ref, f32[8,512]{1,0:T(8,128)S(1)} %copy-done.2, f32[8,64,512]{2,1,0:T(8,128)S(1)} %get-tuple-element.123.field_ref, ...), custom_call_target="tpu_custom_call" | custom-call | tf_op jit(solution)/shard_map/diffuse/pallas_call | solution.py:461
  (8 shorter events, 0.2 us)
Async XLA Ops:
  0.0 15.5 %copy-start.1 = (bf16[64,1024]{1,0:T(8,128)(2,1)S(1)}, bf16[64,1024]{1,0:T(8,128)(2,1)}, u32[]{:S(2)}) copy-start(bf16[64,1024]{1,0:T(8,128)(2,1)} %traces_ref.2) | copy-start | bytes 393220
  0.0 7.2 %copy-start.3 = (s32[64,4]{0,1:T(4,128)S(1)}, s32[64,4]{0,1:T(4,128)}, u32[]{:S(2)}) copy-start(s32[64,4]{0,1:T(4,128)} %param.11) | copy-start | bytes 3076
  0.0 7.3 %copy-start = (f32[64,8,512]{2,1,0:T(8,128)S(1)}, f32[64,8,512]{2,1,0:T(8,128)}, u32[]{:S(2)}) copy-start(f32[64,8,512]{2,1,0:T(8,128)} %param.9) | copy-start | bytes 3145732
  5.0 23.7 %copy-start.2 = (f32[8,512]{1,0:T(8,128)S(1)}, f32[8,512]{1,0:T(8,128)}, u32[]{:S(2)}) copy-start(f32[8,512]{1,0:T(8,128)} %correlation_ref.3) | copy-start | bytes 49156
  5.1 7.2 %collective-permute-start.4 = (f32[104,512]{1,0:T(8,128)S(1)}, f32[104,512]{1,0:T(8,128)S(1)}, u32[]{:S(2)}, u32[]{:S(2)}) collective-permute-start(f32[104,512]{1,0:T(8,128)S(1)} %get-tuple-element.99), channel_id=1, source_target_pairs={{0,4},{4,0},{8,12},{12,8},{1,5},{5,1},{9,13},{13,9},{2,6},{6,2},{1... | collective-permute-start | bytes 638984 | tf_op jit(solution)/shard_map/ppermute | solution.py:507
  12.3 11.6 %collective-permute-start.6 = (f32[104,512]{1,0:T(8,128)S(1)}, f32[104,512]{1,0:T(8,128)S(1)}, u32[]{:S(2)}, u32[]{:S(2)}) collective-permute-start(f32[104,512]{1,0:T(8,128)S(1)} %add.18), channel_id=1, source_target_pairs={{0,12},{4,8},{8,4},{12,0},{1,13},{5,9},{9,5},{13,1},{2,14},{6,10},... | collective-permute-start | bytes 638984 | tf_op jit(solution)/shard_map/ppermute | solution.py:510
  20.0 3.9 %collective-permute-start.5 = (f32[64,512]{1,0:T(8,128)S(1)}, f32[64,512]{1,0:T(8,128)S(1)}, u32[]{:S(2)}, u32[]{:S(2)}) collective-permute-start(f32[64,512]{1,0:T(8,128)S(1)} %get-tuple-element.108), channel_id=1, source_target_pairs={{0,4},{4,0},{8,12},{12,8},{1,5},{5,1},{9,13},{13,9},{2,6},{6,2},{1... | collective-permute-start | bytes 393224 | tf_op jit(solution)/shard_map/ppermute | solution.py:507
  23.9 4.8 %collective-permute-start.9 = (f32[104,512]{1,0:T(8,128)S(1)}, f32[104,512]{1,0:T(8,128)S(1)}, u32[]{:S(2)}, u32[]{:S(2)}) collective-permute-start(f32[104,512]{1,0:T(8,128)S(1)} %add.20), channel_id=1, source_target_pairs={{0,4},{4,0},{8,12},{12,8},{1,5},{5,1},{9,13},{13,9},{2,6},{6,2},{1... | collective-permute-start | bytes 638984 | tf_op jit(solution)/shard_map/ppermute | solution.py:507
  24.4 13.4 %collective-permute-start.7 = (f32[64,512]{1,0:T(8,128)S(1)}, f32[64,512]{1,0:T(8,128)S(1)}, u32[]{:S(2)}, u32[]{:S(2)}) collective-permute-start(f32[64,512]{1,0:T(8,128)S(1)} %add.19), channel_id=1, source_target_pairs={{0,12},{4,8},{8,4},{12,0},{1,13},{5,9},{9,5},{13,1},{2,14},{6,10},... | collective-permute-start | bytes 393224 | tf_op jit(solution)/shard_map/ppermute | solution.py:510
  30.1 14.7 %collective-permute-start.10 = (f32[264,512]{1,0:T(8,128)S(1)}, f32[264,512]{1,0:T(8,128)S(1)}, u32[]{:S(2)}, u32[]{:S(2)}) collective-permute-start(f32[264,512]{1,0:T(8,128)S(1)} %edge_rows.1), channel_id=1, source_target_pairs={{0,0},{1,2},{2,1},{3,3},{4,4},{5,6},{6,5},{7,7},{8,8},{9,10},{10,9... | collective-permute-start | bytes 1622024 | tf_op jit(solution)/shard_map/ppermute | solution.py:513
  37.7 4.5 %collective-permute-start.8 = (f32[64,512]{1,0:T(8,128)S(1)}, f32[64,512]{1,0:T(8,128)S(1)}, u32[]{:S(2)}, u32[]{:S(2)}) collective-permute-start(f32[64,512]{1,0:T(8,128)S(1)} %add.21), channel_id=1, source_target_pairs={{0,4},{4,0},{8,12},{12,8},{1,5},{5,1},{9,13},{13,9},{2,6},{6,2},{1... | collective-permute-start | bytes 393224 | tf_op jit(solution)/shard_map/ppermute | solution.py:507
  44.7 1.9 %collective-permute-start.11 = (f32[264,512]{1,0:T(8,128)S(1)}, f32[264,512]{1,0:T(8,128)S(1)}, u32[]{:S(2)}, u32[]{:S(2)}) collective-permute-start(f32[264,512]{1,0:T(8,128)S(1)} %get-tuple-element.125), channel_id=1, source_target_pairs={{0,1},{1,0},{2,3},{3,2},{4,5},{5,4},{6,7},{7,6},{8,9},{9,8},{10,11... | collective-permute-start | bytes 1622024 | tf_op jit(solution)/shard_map/ppermute | solution.py:559

commit v5 on v4

--- a/solution.py
+++ b/solution.py
@@ -384,12 +384,21 @@
     again = more_ref[0] > 0
     has_above = jnp.where(index > 0, 1.0, 0.0)
     has_below = jnp.where(index < last, 1.0, 0.0)
+
+    inner_at = jnp.where(odd, 0, PASSES)
+    outer_at = PASSES - inner_at
+    has_outer = jnp.where(odd, has_below, has_above)
+    has_inner = jnp.where(odd, has_above, has_below)
     for row in range(PASSES):
         chosen = slice(row * comps, (row + 1) * comps)
-        inner = inner_ref[chosen, :]
-        outer = jnp.where(again, again_ref[chosen, :], outer_ref[chosen, :])
-        edge_ref[row] = has_above * jnp.where(odd, inner, outer)
-        edge_ref[PASSES + row] = has_below * jnp.where(odd, outer, inner)
+        edge_ref[inner_at + row] = has_inner * inner_ref[chosen, :]
+        edge_ref[outer_at + row] = has_outer * outer_ref[chosen, :]
+
+    @pl.when(again)
+    def _():
+        for row in range(PASSES):
+            edge_ref[outer_at + row] = has_outer * again_ref[row * comps : (row + 1) * comps, :]
+
     inner, outer = inner_ref[PASSES * comps :, :], outer_ref[PASSES * comps :, :]
     parts = (
         (0, (diffusion_rate * has_above) * jnp.where(odd, inner, outer)[rows - PASSES :]),
@@ -448,7 +457,7 @@
         copy(step).start()
         return carry
 
-    lax.fori_loop(0, comps // group, relax, 0)
+    lax.fori_loop(0, comps // group, relax, 0, unroll=2)
     for step in range(comps // group):
         copy(step).wait()
 

time: 53.3 us -> 53 us (level)
  no operation moved by 1% of the time
where the time goes in v5:
time: 53 us; the launch traced here: 52.3 us
  Pallas kernels  20.2 us (38%)
  starting transfers between devices  17.4 us (33%)
  waiting for transfers between devices  13.4 us (25%)
  between operations  0.86 us (2%)
    ppermute x4, waiting for transfers between devices, near(): return lax.ppermute(array, 'tm', NEAR)  9.91 us
    pallas_call x2, Pallas kernels, project(): pl.pallas_call(functools.partial(project_kernel, first, chunks), name='pr...  9.42 us
    ppermute x1, starting transfers between devices, beside(): return lax.ppermute(array, 'rows', outside)  7.65 us
    ppermute x2, starting transfers between devices, far(): return lax.ppermute(array, 'tm', FAR)  6.41 us
    pallas_call x1, Pallas kernels, diffuse(): pl.pallas_call(diffuse_kernel, name='diffuse', in_specs=[SCALARS] * 2 + [...  5.65 us
    ppermute x4, starting transfers between devices, near(): return lax.ppermute(array, 'tm', NEAR)  3.37 us
    pallas_call x1, Pallas kernels, plan(): pl.pallas_call(functools.partial(plan_kernel, count), name='plan', in_spe...  1.97 us
    ppermute x1, waiting for transfers between devices, per_device(): inner = lax.ppermute(to_inner, 'rows', inside)  1.93 us
  transfers between devices with their start and end apart: 8, of which 6 were waited for; matrix products, arithmetic and copies ran while one was open for 0% of the time, Pallas kernels for 18%

profile of v5, /device:TPU:1, one launch (start us, length us, event | category | flops | bytes accessed | tf_op | source)
XLA Modules:
  0.0 52.3 jit_solution(7355817304827050136)
XLA Ops:
  0.0 0.0 copy-start.1
  0.0 0.0 copy-start.3
  0.0 0.0 copy-start
  0.0 0.1 pad_add_fusion.where_ref
  0.1 4.9 %project.4 = (f32[104,512]{1,0:T(8,128)S(1)}, f32[104,512]{1,0:T(8,128)S(1)}) custom-call(s32[3]{0:T(128)S(1)} %pad_add_fusion.where_ref, s32[4,64]{1,0:T(4,128)} %bitcast.20, bf16[64,1024]{1,0:T(8,128)(2,1)} %traces_ref.2, bf16[8192,512]{1,0:T(8,128)(2,1)} %bitcast.17), custom_call_target="tpu_custom_call" | custom-call | tf_op jit(solution)/shard_map/project/pallas_call | solution.py:129
  5.0 0.0 copy-start.2
  5.1 2.2 %collective-permute-start.4 = (f32[104,512]{1,0:T(8,128)S(1)}, f32[104,512]{1,0:T(8,128)S(1)}, u32[]{:S(2)}, u32[]{:S(2)}) collective-permute-start(f32[104,512]{1,0:T(8,128)S(1)} %get-tuple-element.99), channel_id=1, source_target_pairs={{0,4},{4,0},{8,12},{12,8},{1,5},{5,1},{9,13},{13,9},{2,6},{6,2},{1... | collective-permute-start | bytes 638984 | tf_op jit(solution)/shard_map/ppermute | solution.py:516
  7.2 0.0 copy-done.3
  7.2 0.1 copy.6.support_ref
  7.3 0.0 copy-done
  7.3 2.0 %plan.1 = (f32[8,64,512]{2,1,0:T(8,128)S(1)}, f32[2,64,128]{2,1,0:T(8,128)S(1)}, bf16[64,256]{1,0:T(8,128)(2,1)S(1)}, bf16[128,256]{1,0:T(8,128)(2,1)S(1)}, bf16[128,256]{1,0:T(8,128)(2,1)S(1)}, /*index=5*/s32[1]{0:T(128)}) custom-call(s32[3]{0:T(128)S(1)} %pad_add_fusion.where_ref, s32[64,4]{1,0:T(8,128)S(1)} %copy.6.support_ref, f32[2048,128]{1,0:T(8,128)S(1)} %bitcast.16), custom_call_target="tpu_custom_call" | custom-call | tf_op jit(solution)/shard_map/plan/pallas_call | solution.py:258
  9.3 2.9 %collective-permute-done.4 = f32[104,512]{1,0:T(8,128)S(1)} collective-permute-done((f32[104,512]{1,0:T(8,128)S(1)}, f32[104,512]{1,0:T(8,128)S(1)}, u32[]{:S(2)}, u32[]{:S(2)}) %collective-permute-start.4) | collective-permute-done | bytes 213024 | tf_op jit(solution)/shard_map/ppermute | solution.py:516
  12.3 3.2 %collective-permute-start.6 = (f32[104,512]{1,0:T(8,128)S(1)}, f32[104,512]{1,0:T(8,128)S(1)}, u32[]{:S(2)}, u32[]{:S(2)}) collective-permute-start(f32[104,512]{1,0:T(8,128)S(1)} %add.18), channel_id=1, source_target_pairs={{0,12},{4,8},{8,4},{12,0},{1,13},{5,9},{9,5},{13,1},{2,14},{6,10},... | collective-permute-start | bytes 638984 | tf_op jit(solution)/shard_map/ppermute | solution.py:519
  15.5 0.0 copy-done.1
  15.5 4.5 %project.5 = (f32[64,512]{1,0:T(8,128)S(1)}, f32[64,512]{1,0:T(8,128)S(1)}) custom-call(s32[3]{0:T(128)S(1)} %pad_add_fusion.where_ref, s32[4,64]{1,0:T(4,128)S(1)} %bitcast.21, bf16[64,1024]{1,0:T(8,128)(2,1)S(1)} %copy-done.1, bf16[8192,512]{1,0:T(8,128)(2,1)} %bitcast.18), custom_call_target="tpu_custom_call" | custom-call | tf_op jit(solution)/shard_map/project/pallas_call | solution.py:129
  20.0 0.1 collective-permute-start.5
  20.1 3.8 %collective-permute-done.5 = f32[64,512]{1,0:T(8,128)S(1)} collective-permute-done((f32[64,512]{1,0:T(8,128)S(1)}, f32[64,512]{1,0:T(8,128)S(1)}, u32[]{:S(2)}, u32[]{:S(2)}) %collective-permute-start.5) | collective-permute-done | bytes 131104 | tf_op jit(solution)/shard_map/ppermute | solution.py:516
  23.9 0.0 collective-permute-done.6
  23.9 0.4 collective-permute-start.9
  24.4 3.2 %collective-permute-start.7 = (f32[64,512]{1,0:T(8,128)S(1)}, f32[64,512]{1,0:T(8,128)S(1)}, u32[]{:S(2)}, u32[]{:S(2)}) collective-permute-start(f32[64,512]{1,0:T(8,128)S(1)} %add.19), channel_id=1, source_target_pairs={{0,12},{4,8},{8,4},{12,0},{1,13},{5,9},{9,5},{13,1},{2,14},{6,10},... | collective-permute-start | bytes 393224 | tf_op jit(solution)/shard_map/ppermute | solution.py:519
  27.5 1.2 %collective-permute-done.9 = f32[104,512]{1,0:T(8,128)S(1)} collective-permute-done((f32[104,512]{1,0:T(8,128)S(1)}, f32[104,512]{1,0:T(8,128)S(1)}, u32[]{:S(2)}, u32[]{:S(2)}) %collective-permute-start.9) | collective-permute-done | bytes 213024 | tf_op jit(solution)/shard_map/ppermute | solution.py:516
  28.8 0.0 copy-done.2
  28.8 1.3 %edge_rows.1 = f32[264,512]{1,0:T(8,128)S(1)} custom-call(s32[3]{0:T(128)S(1)} %pad_add_fusion.where_ref, f32[208,512]{1,0:T(8,128)S(1)} %pad_maximum_fusion.1.sums_ref, f32[8,64,512]{2,1,0:T(8,128)S(1)} %get-tuple-element.114.planes_ref, f32[2,64,128]{2,1,0:T(8,128)S(1)} %get-tuple-element.102.act_ref, bf16[64,256]{1,0:T(8,128)(2,1)S(1)} %get-tuple-element.113.first_ref, ...), custom_call_target="tpu_custom_call" | custom-call | tf_op jit(solution)/shard_map/edge_rows/pallas_call | solution.py:290
  30.1 7.6 %collective-permute-start.10 = (f32[264,512]{1,0:T(8,128)S(1)}, f32[264,512]{1,0:T(8,128)S(1)}, u32[]{:S(2)}, u32[]{:S(2)}) collective-permute-start(f32[264,512]{1,0:T(8,128)S(1)} %edge_rows.1), channel_id=1, source_target_pairs={{0,0},{1,2},{2,1},{3,3},{4,4},{5,6},{6,5},{7,7},{8,8},{9,10},{10,9... | collective-permute-start | bytes 1622024 | tf_op jit(solution)/shard_map/ppermute | solution.py:522
  37.7 0.0 collective-permute-done.7
  37.7 0.7 %collective-permute-start.8 = (f32[64,512]{1,0:T(8,128)S(1)}, f32[64,512]{1,0:T(8,128)S(1)}, u32[]{:S(2)}, u32[]{:S(2)}) collective-permute-start(f32[64,512]{1,0:T(8,128)S(1)} %add.21), channel_id=1, source_target_pairs={{0,4},{4,0},{8,12},{12,8},{1,5},{5,1},{9,13},{13,9},{2,6},{6,2},{1... | collective-permute-start | bytes 393224 | tf_op jit(solution)/shard_map/ppermute | solution.py:516
  39.1 1.0 %prepare.1 = (f32[8,64,512]{2,1,0:T(8,128)S(1)}, f32[64,128]{1,0:T(8,128)S(1)}) custom-call(f32[208,512]{1,0:T(8,128)S(1)} %pad_maximum_fusion.1.sums_ref, f32[8,64,512]{2,1,0:T(8,128)S(1)} %get-tuple-element.114.planes_ref, f32[2,64,128]{2,1,0:T(8,128)S(1)} %get-tuple-element.102.act_ref), custom_call_target="tpu_custom_call" | custom-call | tf_op jit(solution)/shard_map/prepare/pallas_call | solution.py:309
  40.2 2.0 %collective-permute-done.8 = f32[64,512]{1,0:T(8,128)S(1)} collective-permute-done((f32[64,512]{1,0:T(8,128)S(1)}, f32[64,512]{1,0:T(8,128)S(1)}, u32[]{:S(2)}, u32[]{:S(2)}) %collective-permute-start.8) | collective-permute-done | bytes 131104 | tf_op jit(solution)/shard_map/ppermute | solution.py:516
  42.3 0.9 %conditional.1 = ((f32[8,64,512]{2,1,0:T(8,128)S(1)}, f32[264,512]{1,0:T(8,128)S(1)}, f32[264,512]{1,0:T(8,128)S(1)})) conditional(s32[]{:T(128)} %bitcast.8, (s32[3]{0:T(128)S(1)}, f32[8,64,512]{2,1,0:T(8,128)S(1)}, bf16[128,256]{1,0:T(8,128)(2,1)S(1)}, bf16[128,256]{1,0:T(8,128)(2,1)S(1)}, f32[64,128]{1,0:T(8,128)S(1)}, ...), branch_computations={%region_0.1_spmd, %region_1.2_spmd} | conditional | flops 827392 | bytes 11534529 | solution.py:566
  42.3 0.9 %step_rows.2 = (f32[8,64,512]{2,1,0:T(8,128)S(1)}, f32[264,512]{1,0:T(8,128)S(1)}, f32[264,512]{1,0:T(8,128)S(1)}) custom-call(s32[3]{0:T(128)S(1)} %get-tuple-element.45.where_ref, f32[8,64,512]{2,1,0:T(8,128)S(1)} %get-tuple-element.46.base_ref, bf16[128,256]{1,0:T(8,128)(2,1)S(1)} %get-tuple-element.47.pick_ref, ...), custom_call_target="tpu_custom_call" | custom-call | tf_op jit(solution)/shard_map/cond/branch_0_fun/step_rows/pallas_call | solution.py:352
  43.2 1.5 %collective-permute-done.10.outer_ref = f32[264,512]{1,0:T(8,128)S(1)} collective-permute-done((f32[264,512]{1,0:T(8,128)S(1)}, f32[264,512]{1,0:T(8,128)S(1)}, u32[]{:S(2)}, u32[]{:S(2)}) %collective-permute-start.10) | collective-permute-done | bytes 540704 | tf_op jit(solution)/shard_map/ppermute | solution.py:522
  44.7 0.0 collective-permute-start.11
  44.7 1.9 %collective-permute-done.11.inner_ref = f32[264,512]{1,0:T(8,128)S(1)} collective-permute-done((f32[264,512]{1,0:T(8,128)S(1)}, f32[264,512]{1,0:T(8,128)S(1)}, u32[]{:S(2)}, u32[]{:S(2)}) %collective-permute-start.11) | collective-permute-done | bytes 540704 | tf_op jit(solution)/shard_map/ppermute | solution.py:568
  46.7 5.6 %diffuse.1 = f32[2048,128]{1,0:T(8,128)} custom-call(s32[3]{0:T(128)S(1)} %pad_add_fusion.where_ref, s32[1]{0:T(128)} %get-tuple-element.101.more_ref, f32[2,64,128]{2,1,0:T(8,128)S(1)} %get-tuple-element.102.act_ref, f32[8,512]{1,0:T(8,128)S(1)} %copy-done.2, f32[8,64,512]{2,1,0:T(8,128)S(1)} %get-tuple-element.123.field_ref, ...), custom_call_target="tpu_custom_call" | custom-call | tf_op jit(solution)/shard_map/diffuse/pallas_call | solution.py:470
  (8 shorter events, 0.2 us)
Async XLA Ops:
  0.0 15.5 %copy-start.1 = (bf16[64,1024]{1,0:T(8,128)(2,1)S(1)}, bf16[64,1024]{1,0:T(8,128)(2,1)}, u32[]{:S(2)}) copy-start(bf16[64,1024]{1,0:T(8,128)(2,1)} %traces_ref.2) | copy-start | bytes 393220
  0.0 7.2 %copy-start.3 = (s32[64,4]{0,1:T(4,128)S(1)}, s32[64,4]{0,1:T(4,128)}, u32[]{:S(2)}) copy-start(s32[64,4]{0,1:T(4,128)} %param.11) | copy-start | bytes 3076
  0.0 7.3 %copy-start = (f32[64,8,512]{2,1,0:T(8,128)S(1)}, f32[64,8,512]{2,1,0:T(8,128)}, u32[]{:S(2)}) copy-start(f32[64,8,512]{2,1,0:T(8,128)} %param.9) | copy-start | bytes 3145732
  5.0 23.7 %copy-start.2 = (f32[8,512]{1,0:T(8,128)S(1)}, f32[8,512]{1,0:T(8,128)}, u32[]{:S(2)}) copy-start(f32[8,512]{1,0:T(8,128)} %correlation_ref.3) | copy-start | bytes 49156
  5.1 7.2 %collective-permute-start.4 = (f32[104,512]{1,0:T(8,128)S(1)}, f32[104,512]{1,0:T(8,128)S(1)}, u32[]{:S(2)}, u32[]{:S(2)}) collective-permute-start(f32[104,512]{1,0:T(8,128)S(1)} %get-tuple-element.99), channel_id=1, source_target_pairs={{0,4},{4,0},{8,12},{12,8},{1,5},{5,1},{9,13},{13,9},{2,6},{6,2},{1... | collective-permute-start | bytes 638984 | tf_op jit(solution)/shard_map/ppermute | solution.py:516
  12.3 11.6 %collective-permute-start.6 = (f32[104,512]{1,0:T(8,128)S(1)}, f32[104,512]{1,0:T(8,128)S(1)}, u32[]{:S(2)}, u32[]{:S(2)}) collective-permute-start(f32[104,512]{1,0:T(8,128)S(1)} %add.18), channel_id=1, source_target_pairs={{0,12},{4,8},{8,4},{12,0},{1,13},{5,9},{9,5},{13,1},{2,14},{6,10},... | collective-permute-start | bytes 638984 | tf_op jit(solution)/shard_map/ppermute | solution.py:519
  20.0 3.9 %collective-permute-start.5 = (f32[64,512]{1,0:T(8,128)S(1)}, f32[64,512]{1,0:T(8,128)S(1)}, u32[]{:S(2)}, u32[]{:S(2)}) collective-permute-start(f32[64,512]{1,0:T(8,128)S(1)} %get-tuple-element.108), channel_id=1, source_target_pairs={{0,4},{4,0},{8,12},{12,8},{1,5},{5,1},{9,13},{13,9},{2,6},{6,2},{1... | collective-permute-start | bytes 393224 | tf_op jit(solution)/shard_map/ppermute | solution.py:516
  23.9 4.8 %collective-permute-start.9 = (f32[104,512]{1,0:T(8,128)S(1)}, f32[104,512]{1,0:T(8,128)S(1)}, u32[]{:S(2)}, u32[]{:S(2)}) collective-permute-start(f32[104,512]{1,0:T(8,128)S(1)} %add.20), channel_id=1, source_target_pairs={{0,4},{4,0},{8,12},{12,8},{1,5},{5,1},{9,13},{13,9},{2,6},{6,2},{1... | collective-permute-start | bytes 638984 | tf_op jit(solution)/shard_map/ppermute | solution.py:516
  24.4 13.4 %collective-permute-start.7 = (f32[64,512]{1,0:T(8,128)S(1)}, f32[64,512]{1,0:T(8,128)S(1)}, u32[]{:S(2)}, u32[]{:S(2)}) collective-permute-start(f32[64,512]{1,0:T(8,128)S(1)} %add.19), channel_id=1, source_target_pairs={{0,12},{4,8},{8,4},{12,0},{1,13},{5,9},{9,5},{13,1},{2,14},{6,10},... | collective-permute-start | bytes 393224 | tf_op jit(solution)/shard_map/ppermute | solution.py:519
  30.1 14.7 %collective-permute-start.10 = (f32[264,512]{1,0:T(8,128)S(1)}, f32[264,512]{1,0:T(8,128)S(1)}, u32[]{:S(2)}, u32[]{:S(2)}) collective-permute-start(f32[264,512]{1,0:T(8,128)S(1)} %edge_rows.1), channel_id=1, source_target_pairs={{0,0},{1,2},{2,1},{3,3},{4,4},{5,6},{6,5},{7,7},{8,8},{9,10},{10,9... | collective-permute-start | bytes 1622024 | tf_op jit(solution)/shard_map/ppermute | solution.py:522
  37.7 4.5 %collective-permute-start.8 = (f32[64,512]{1,0:T(8,128)S(1)}, f32[64,512]{1,0:T(8,128)S(1)}, u32[]{:S(2)}, u32[]{:S(2)}) collective-permute-start(f32[64,512]{1,0:T(8,128)S(1)} %add.21), channel_id=1, source_target_pairs={{0,4},{4,0},{8,12},{12,8},{1,5},{5,1},{9,13},{13,9},{2,6},{6,2},{1... | collective-permute-start | bytes 393224 | tf_op jit(solution)/shard_map/ppermute | solution.py:516
  44.7 1.9 %collective-permute-start.11 = (f32[264,512]{1,0:T(8,128)S(1)}, f32[264,512]{1,0:T(8,128)S(1)}, u32[]{:S(2)}, u32[]{:S(2)}) collective-permute-start(f32[264,512]{1,0:T(8,128)S(1)} %get-tuple-element.125), channel_id=1, source_target_pairs={{0,1},{1,0},{2,3},{3,2},{4,5},{5,4},{6,7},{7,6},{8,9},{9,8},{10,11... | collective-permute-start | bytes 1622024 | tf_op jit(solution)/shard_map/ppermute | solution.py:568
